TPU v7x, 256 devices: a whole 4x4x8 slice. The times are simulated.
256 devices in a mesh: sec: 8 (over z), chan: 32 (over y, x, core).
Axes of the slice: x: 4, y: 4, z: 8, core: 2. Of those that a mesh axis runs over, the one named last changes fastest.
Arguments:
- state_blocks: bfloat16 [8, 512, 512], P('sec'), may hold values from -6 to 6
- left_blocks: bfloat16 [256, 8, 512, 512], P('chan', 'sec'), may hold values from -0.25 to 0.25
- right_blocks: bfloat16 [256, 8, 512, 512], P('chan', 'sec'), may hold values from -0.25 to 0.25
- widths: int32 [8], P('sec'), may hold values from 128 to 512
- step_sizes: float32 [8], P('sec'), may hold values from 0.1 to 0.4
- shifts: int32 [256], P('chan'), may hold values from -1 to 1
Outputs:
- update: bfloat16 [8, 512, 512], P('sec', 'chan')
- new_left: bfloat16 [256, 8, 512, 512], P('chan', 'sec')
All inputs are finite; a program needn't handle non-finite values.
Results may differ from a plain program's by a relative error of at most 0.012.
Values may be sent and summed in bfloat16 or wider, within the bound.
A program may use at most 64 MiB of HBM per device.

v0:
```python
import jax
import jax.numpy as jnp
from jax import lax
from jax.sharding import PartitionSpec as P

REACH = 1


def padded_2(shard, sides, width):
    for axis, dim in sides:
        count, length = (lax.axis_size(axis), shard.shape[dim])
        up = [(i, (i + 1) % count) for i in range(count - 1)]
        down = [(j, i) for i, j in up]
        last = lax.slice_in_dim(shard, length - width, length, axis=dim)
        initial = lax.slice_in_dim(shard, 0, width, axis=dim)
        before = lax.ppermute(last, axis, up)
        after = lax.ppermute(initial, axis, down)
        shard = jnp.concatenate([before, shard, after], axis=dim)
    return shard


def in_blocks(shard, dim, count):
    dims = shard.shape
    tiles = shard.reshape(*dims[:dim], count, dims[dim] // count, *dims[dim + 1 :])
    return jnp.moveaxis(tiles, dim, 0)


def sent_and_summed(shard, axis, dim):
    tiles = in_blocks(shard, dim, lax.axis_size(axis))
    arrived = lax.all_to_all(tiles, axis, split_axis=0, concat_axis=0, tiled=True)
    return arrived.astype(jnp.float32).sum(axis=0)


def from_everyone(shard, axis):
    count = lax.axis_size(axis)
    return lax.all_to_all(
        jnp.broadcast_to(shard[None], (count, *shard.shape)), axis, 0, 0, tiled=True
    )


def joined_along(tiles, dim):
    dims = list(tiles.shape[1:])
    dims[dim] *= tiles.shape[0]
    return jnp.moveaxis(tiles, 0, dim).reshape(dims)


def gather_directly(shard, axis, dim):
    tiles = from_everyone(shard, axis)
    return joined_along(tiles, dim)


def padded_term(left, right, source):
    halfway = jnp.dot(left, source, preferred_element_type=jnp.float32).astype(jnp.bfloat16)
    return lax.dot_general(
        halfway, right, (((1,), (1,)), ((), ())), preferred_element_type=jnp.float32
    )


def shards(state_blocks, left_blocks, right_blocks, widths, step_sizes, shifts):
    padded = state_blocks.shape[1]
    chan_count = left_blocks.shape[0]
    positions = jnp.arange(padded, dtype=jnp.int32)
    within = positions[None, :] < widths[:, None]
    inside = within[:, :, None] & within[:, None, :]
    states = jnp.where(inside, state_blocks, jnp.zeros_like(state_blocks))
    extended = padded_2(states, (("sec", 0),), REACH)
    sector = 0
    total = jnp.zeros((padded, padded), jnp.float32)
    for channel in range(chan_count):
        offset = shifts[channel]
        source = lax.dynamic_slice_in_dim(extended, sector + REACH - offset, 1, 0)[0]
        left = left_blocks[channel, sector]
        right = right_blocks[channel, sector]
        total = total + padded_term(left, right, source)
    sector_sums = [total]
    partial_sum = jnp.stack(sector_sums)
    share_rows = padded // lax.axis_size("chan")
    row_start = lax.axis_index("chan") * share_rows
    summed_rows = sent_and_summed(partial_sum.astype(jnp.bfloat16), "chan", 1)
    inside_rows = lax.dynamic_slice_in_dim(inside, row_start, share_rows, 1)
    state_rows = lax.dynamic_slice_in_dim(states, row_start, share_rows, 1)
    product_rows = jnp.where(inside_rows, summed_rows, jnp.zeros_like(summed_rows))
    corrected = state_rows.astype(jnp.float32) - step_sizes[:, None, None] * product_rows
    update_rows = jnp.where(inside_rows, corrected, jnp.zeros_like(corrected)).astype(jnp.bfloat16)
    update = gather_directly(update_rows, "chan", 1)
    update_ext = padded_2(update, (("sec", 0),), REACH)
    norm_factor = padded ** (-0.5)
    channel_rows = []
    for channel in range(chan_count):
        offset = shifts[channel]
        sector = 0
        ket_block = lax.dynamic_slice_in_dim(update_ext, sector + REACH - offset, 1, 0)[0]
        pulled = jnp.dot(
            left_blocks[channel, sector], ket_block, preferred_element_type=jnp.float32
        ).astype(jnp.bfloat16)
        rotated = lax.dot_general(
            update[sector], pulled, (((0,), (0,)), ((), ())), preferred_element_type=jnp.float32
        )
        rotated_list = [(rotated * norm_factor).astype(jnp.bfloat16)]
        channel_rows.append(jnp.stack(rotated_list))
    new_left = jnp.stack(channel_rows)
    return (update_rows, new_left)


def solution(mesh):
    placed = (
        P("sec", None, None),
        P("chan", "sec", None, None),
        P("chan", "sec", None, None),
        P("sec"),
        P("sec"),
        P("chan"),
    )
    return jax.shard_map(
        shards,
        mesh=mesh,
        in_specs=placed,
        out_specs=(P("sec", "chan", None), P("chan", "sec", None, None)),
        check_vma=False,
    )
```

profile of v0, /device:TPU:128, one launch (start us, length us, event | category | flops | bytes accessed | tf_op | source)
XLA Modules:
  0.0 119.2 jit_solution(7937685976265867039)
XLA Ops:
  1.3 1.3 %broadcast_select_fusion = bf16[1,512,512]{2,1,0:T(8,128)(2,1)S(1)} fusion(bf16[1,512,512]{2,1,0:T(8,128)(2,1)} %param.6, pred[512]{0:T(512)(128)(4,1)S(1)} %iota_compare_fusion), kind=kLoop, calls=%fused_computation.141 | loop fusion | flops 524288 | bytes 1049088 | tf_op jit(solution)/shard_map/jit(_where)/select_n | solution.py:65
  2.6 2.0 %collective-permute-start.1 = (bf16[1,512,512]{2,1,0:T(8,128)(2,1)S(1)}, bf16[1,512,512]{2,1,0:T(8,128)(2,1)S(1)}, u32[]{:S(2)}, u32[]{:S(2)}) collective-permute-start(bf16[1,512,512]{2,1,0:T(8,128)(2,1)S(1)} %broadcast_select_fusion), channel_id=1, source_target_pairs={{32,0},{64,32},{96,64},{128,96},{160,128},{192,160},{224,192},{33,... | collective-permute-start | bytes 1572872 | tf_op jit(solution)/shard_map/ppermute | solution.py:17
  4.6 3.8 %collective-permute-start = (bf16[1,512,512]{2,1,0:T(8,128)(2,1)S(1)}, bf16[1,512,512]{2,1,0:T(8,128)(2,1)S(1)}, u32[]{:S(2)}, u32[]{:S(2)}) collective-permute-start(bf16[1,512,512]{2,1,0:T(8,128)(2,1)S(1)} %broadcast_select_fusion), channel_id=1, source_target_pairs={{0,32},{32,64},{64,96},{96,128},{128,160},{160,192},{192,224},{1,3... | collective-permute-start | bytes 1572872 | tf_op jit(solution)/shard_map/ppermute | solution.py:16
  8.4 1.6 %fusion.206 = (s32[1]{0:T(128)}, s32[1]{0:T(128)}, s32[1]{0:T(128)}, s32[1]{0:T(128)}, s32[1]{0:T(128)}, /*index=5*/s32[1]{0:T(128)}, s32[1]{0:T(128)}, s32[1]{0:T(128)}) fusion(s32[8]{0:T(128)} %param.11), kind=kLoop, calls=%fused_computation.164 | loop fusion | bytes 64 | tf_op jit(solution)/shard_map/slice | solution.py:70
  19.9 0.0 collective-permute-done.1
  19.9 1.3 %collective-permute-done = bf16[1,512,512]{2,1,0:T(8,128)(2,1)S(1)} collective-permute-done((bf16[1,512,512]{2,1,0:T(8,128)(2,1)S(1)}, bf16[1,512,512]{2,1,0:T(8,128)(2,1)S(1)}, u32[]{:S(2)}, u32[]{:S(2)}) %collective-permute-start) | collective-permute-done | bytes 524320 | tf_op jit(solution)/shard_map/ppermute | solution.py:16
  21.3 0.2 pad_maximum_fusion
  21.4 3.0 %fusion.25 = f32[512,512]{1,0:T(8,128)} fusion(bf16[8,1,512,512]{3,2,1,0:T(8,128)(2,1)} %param.8, bf16[3,512,512]{2,1,0:T(8,128)(2,1)S(1)} %pad_maximum_fusion, s32[]{:T(128)S(6)} %select_n.49, bf16[8,1,512,512]{3,2,1,0:T(8,128)(2,1)} %param.7), kind=kOutput, calls=%fused_computation.58 | convolution fusion | flops 537133056 | bytes 2621444 | tf_op jit(solution)/shard_map/dot_general | solution.py:54
  24.5 2.4 %convolution_add_fusion.6 = f32[512,512]{1,0:T(8,128)S(1)} fusion(f32[512,512]{1,0:T(8,128)} %fusion.25, bf16[8,1,512,512]{3,2,1,0:T(8,128)(2,1)} %param.8, bf16[3,512,512]{2,1,0:T(8,128)(2,1)S(1)} %pad_maximum_fusion, s32[]{:T(128)S(6)} %select_n.50, bf16[8,1,512,512]{3,2,1,0:T(8,128)(2,1)} %param.7), kind=kOutput, calls=%fused_computation.16 | convolution fusion | flops 537395200 | bytes 3670020 | tf_op jit(solution)/shard_map/dot_general | solution.py:54
  26.9 3.0 %convolution_add_fusion.5 = f32[512,512]{1,0:T(8,128)} fusion(f32[512,512]{1,0:T(8,128)S(1)} %convolution_add_fusion.6, bf16[8,1,512,512]{3,2,1,0:T(8,128)(2,1)} %param.8, bf16[3,512,512]{2,1,0:T(8,128)(2,1)S(1)} %pad_maximum_fusion, s32[]{:T(128)S(6)} %select_n.51, bf16[8,1,512,512]{3,2,1,0:T(8,128)(2,1)} %param.7), kind=kOutput, calls=%fused_computation.15 | convolution fusion | flops 537395200 | bytes 3670020 | tf_op jit(solution)/shard_map/dot_general | solution.py:54
  29.9 2.4 %convolution_add_fusion.4 = f32[512,512]{1,0:T(8,128)S(1)} fusion(f32[512,512]{1,0:T(8,128)} %convolution_add_fusion.5, bf16[8,1,512,512]{3,2,1,0:T(8,128)(2,1)} %param.8, bf16[3,512,512]{2,1,0:T(8,128)(2,1)S(1)} %pad_maximum_fusion, s32[]{:T(128)S(6)} %select_n.52, bf16[8,1,512,512]{3,2,1,0:T(8,128)(2,1)} %param.7), kind=kOutput, calls=%fused_computation.14 | convolution fusion | flops 537395200 | bytes 3670020 | tf_op jit(solution)/shard_map/dot_general | solution.py:54
  32.4 3.0 %convolution_add_fusion.3 = f32[512,512]{1,0:T(8,128)} fusion(f32[512,512]{1,0:T(8,128)S(1)} %convolution_add_fusion.4, bf16[8,1,512,512]{3,2,1,0:T(8,128)(2,1)} %param.8, bf16[3,512,512]{2,1,0:T(8,128)(2,1)S(1)} %pad_maximum_fusion, s32[]{:T(128)S(6)} %select_n.53, bf16[8,1,512,512]{3,2,1,0:T(8,128)(2,1)} %param.7), kind=kOutput, calls=%fused_computation.13 | convolution fusion | flops 537395200 | bytes 3670020 | tf_op jit(solution)/shard_map/dot_general | solution.py:54
  35.4 2.4 %convolution_add_fusion.2 = f32[512,512]{1,0:T(8,128)S(1)} fusion(f32[512,512]{1,0:T(8,128)} %convolution_add_fusion.3, bf16[8,1,512,512]{3,2,1,0:T(8,128)(2,1)} %param.8, bf16[3,512,512]{2,1,0:T(8,128)(2,1)S(1)} %pad_maximum_fusion, s32[]{:T(128)S(6)} %select_n.54, bf16[8,1,512,512]{3,2,1,0:T(8,128)(2,1)} %param.7), kind=kOutput, calls=%fused_computation.12 | convolution fusion | flops 537395200 | bytes 3670020 | tf_op jit(solution)/shard_map/dot_general | solution.py:54
  37.8 3.0 %convolution_add_fusion.1 = f32[512,512]{1,0:T(8,128)} fusion(f32[512,512]{1,0:T(8,128)S(1)} %convolution_add_fusion.2, bf16[8,1,512,512]{3,2,1,0:T(8,128)(2,1)} %param.8, bf16[3,512,512]{2,1,0:T(8,128)(2,1)S(1)} %pad_maximum_fusion, s32[]{:T(128)S(6)} %select_n.55, bf16[8,1,512,512]{3,2,1,0:T(8,128)(2,1)} %param.7), kind=kOutput, calls=%fused_computation.11 | convolution fusion | flops 537395200 | bytes 3670020 | tf_op jit(solution)/shard_map/dot_general | solution.py:54
  40.9 3.2 %fusion = bf16[512,512]{1,0:T(8,128)(2,1)} fusion(f32[512,512]{1,0:T(8,128)} %convolution_add_fusion.1, bf16[8,1,512,512]{3,2,1,0:T(8,128)(2,1)} %param.8, bf16[3,512,512]{2,1,0:T(8,128)(2,1)S(1)} %pad_maximum_fusion, s32[]{:T(128)S(6)} %select_n.56, bf16[8,1,512,512]{3,2,1,0:T(8,128)(2,1)} %param.7), kind=kOutput, calls=%fused_computation.33 | convolution fusion | flops 537657344 | bytes 3145732 | tf_op jit(solution)/shard_map/dot_general | solution.py:54
  44.1 7.3 %all-to-all-start = ((bf16[32,1,16,512]{3,2,1,0:T(8,128)(2,1)}), bf16[32,1,16,512]{3,2,1,0:T(8,128)(2,1)S(1)}, u32[]{:S(2)}, u32[]{:S(2)}) async-start(bf16[32,1,16,512]{3,2,1,0:T(8,128)(2,1)} %bitcast.43), calls=%async_computation | async-start | bytes 1048576 | tf_op jit(solution)/shard_map/all_to_all | solution.py:30
  52.1 0.2 broadcast_and_fusion
  52.2 10.9 %all-to-all-done = bf16[32,1,16,512]{3,2,1,0:T(8,128)(2,1)S(1)} async-done(((bf16[32,1,16,512]{3,2,1,0:T(8,128)(2,1)}), bf16[32,1,16,512]{3,2,1,0:T(8,128)(2,1)S(1)}, u32[]{:S(2)}, u32[]{:S(2)}) %all-to-all-start) | async-done | bytes 524320 | tf_op jit(solution)/shard_map/all_to_all | solution.py:30
  63.2 0.1 convert_reduce_fusion
  63.3 0.0 copy-start
  63.3 0.1 broadcast_in_dim.8
  63.3 15.2 %all_to_all.10 = bf16[32,1,16,512]{3,2,1,0:T(8,128)(2,1)S(1)} all-to-all(bf16[32,1,16,512]{3,2,1,0:T(8,128)(2,1)S(1)} %broadcast_in_dim.8), channel_id=1, replica_groups=mesh['sec'=8,'chan'=32] {'chan'}, dimensions={0} | all-to-all | bytes 1048576 | tf_op jit(solution)/shard_map/all_to_all | solution.py:36
  78.6 1.9 %collective-permute-start.3 = (bf16[1,512,512]{2,1,0:T(8,128)(2,1)S(1)}, bf16[1,512,512]{2,1,0:T(8,128)(2,1)S(1)}, u32[]{:S(2)}, u32[]{:S(2)}) collective-permute-start(bf16[1,512,512]{2,1,0:T(8,128)(2,1)S(1)} %bitcast.220), channel_id=1, source_target_pairs={{32,0},{64,32},{96,64},{128,96},{160,128},{192,160},{224,192},{33,... | collective-permute-start | bytes 1572872 | tf_op jit(solution)/shard_map/ppermute | solution.py:17
  80.5 4.1 %collective-permute-start.2 = (bf16[1,512,512]{2,1,0:T(8,128)(2,1)S(1)}, bf16[1,512,512]{2,1,0:T(8,128)(2,1)S(1)}, u32[]{:S(2)}, u32[]{:S(2)}) collective-permute-start(bf16[1,512,512]{2,1,0:T(8,128)(2,1)S(1)} %bitcast.221), channel_id=1, source_target_pairs={{0,32},{32,64},{64,96},{96,128},{128,160},{160,192},{192,224},{1,3... | collective-permute-start | bytes 1572872 | tf_op jit(solution)/shard_map/ppermute | solution.py:16
  84.6 9.7 %collective-permute-done.3 = bf16[1,512,512]{2,1,0:T(8,128)(2,1)S(1)} collective-permute-done((bf16[1,512,512]{2,1,0:T(8,128)(2,1)S(1)}, bf16[1,512,512]{2,1,0:T(8,128)(2,1)S(1)}, u32[]{:S(2)}, u32[]{:S(2)}) %collective-permute-start.3) | collective-permute-done | bytes 524320 | tf_op jit(solution)/shard_map/ppermute | solution.py:17
  94.3 3.1 %collective-permute-done.2 = bf16[1,512,512]{2,1,0:T(8,128)(2,1)S(1)} collective-permute-done((bf16[1,512,512]{2,1,0:T(8,128)(2,1)S(1)}, bf16[1,512,512]{2,1,0:T(8,128)(2,1)S(1)}, u32[]{:S(2)}, u32[]{:S(2)}) %collective-permute-start.2) | collective-permute-done | bytes 524320 | tf_op jit(solution)/shard_map/ppermute | solution.py:16
  97.5 0.2 pad_maximum_fusion.1
  97.7 2.7 %fusion.24 = bf16[8,1,512,512]{3,2,1,0:T(8,128)(2,1)} fusion(bf16[512,512]{1,0:T(8,128)(2,1)S(1)} %bitcast.223, bf16[3,512,512]{2,1,0:T(8,128)(2,1)S(1)} %pad_maximum_fusion.1, s32[]{:T(128)S(6)} %select_n.49, bf16[8,1,512,512]{3,2,1,0:T(8,128)(2,1)} %param.7), kind=kOutput, calls=%fused_computation.57 | convolution fusion | flops 537657344 | bytes 2097156 | tf_op jit(solution)/shard_map/dot_general | solution.py:96
  100.3 2.7 %fusion.22 = bf16[8,1,512,512]{3,2,1,0:T(8,128)(2,1)} fusion(bf16[8,1,512,512]{3,2,1,0:T(8,128)(2,1)} %fusion.24, bf16[512,512]{1,0:T(8,128)(2,1)S(1)} %bitcast.224, bf16[3,512,512]{2,1,0:T(8,128)(2,1)S(1)} %pad_maximum_fusion.1, s32[]{:T(128)S(6)} %select_n.50, bf16[8,1,512,512]{3,2,1,0:T(8,128)(2,1)} %param.7), kind=kOutput, calls=%fused_computation.55 | convolution fusion | flops 537657344 | bytes 2097156 | tf_op jit(solution)/shard_map/dot_general | solution.py:96
  103.0 0.0 copy-done
  103.0 2.7 %fusion.20 = bf16[8,1,512,512]{3,2,1,0:T(8,128)(2,1)} fusion(bf16[8,1,512,512]{3,2,1,0:T(8,128)(2,1)} %fusion.22, bf16[512,512]{1,0:T(8,128)(2,1)S(1)} %bitcast.225, bf16[3,512,512]{2,1,0:T(8,128)(2,1)S(1)} %pad_maximum_fusion.1, s32[]{:T(128)S(6)} %select_n.51, bf16[8,1,512,512]{3,2,1,0:T(8,128)(2,1)} %param.7), kind=kOutput, calls=%fused_computation.53 | convolution fusion | flops 537657344 | bytes 2097156 | tf_op jit(solution)/shard_map/dot_general | solution.py:96
  105.7 2.7 %fusion.18 = bf16[8,1,512,512]{3,2,1,0:T(8,128)(2,1)} fusion(bf16[8,1,512,512]{3,2,1,0:T(8,128)(2,1)} %fusion.20, bf16[512,512]{1,0:T(8,128)(2,1)S(1)} %bitcast.226, bf16[3,512,512]{2,1,0:T(8,128)(2,1)S(1)} %pad_maximum_fusion.1, s32[]{:T(128)S(6)} %select_n.52, bf16[8,1,512,512]{3,2,1,0:T(8,128)(2,1)} %param.7), kind=kOutput, calls=%fused_computation.51 | convolution fusion | flops 537657344 | bytes 2097156 | tf_op jit(solution)/shard_map/dot_general | solution.py:96
  108.4 2.7 %fusion.16 = bf16[8,1,512,512]{3,2,1,0:T(8,128)(2,1)} fusion(bf16[8,1,512,512]{3,2,1,0:T(8,128)(2,1)} %fusion.18, bf16[512,512]{1,0:T(8,128)(2,1)S(1)} %bitcast.227, bf16[3,512,512]{2,1,0:T(8,128)(2,1)S(1)} %pad_maximum_fusion.1, s32[]{:T(128)S(6)} %select_n.53, bf16[8,1,512,512]{3,2,1,0:T(8,128)(2,1)} %param.7), kind=kOutput, calls=%fused_computation.49 | convolution fusion | flops 537657344 | bytes 2097156 | tf_op jit(solution)/shard_map/dot_general | solution.py:96
  111.1 2.7 %fusion.14 = bf16[8,1,512,512]{3,2,1,0:T(8,128)(2,1)} fusion(bf16[8,1,512,512]{3,2,1,0:T(8,128)(2,1)} %fusion.16, bf16[512,512]{1,0:T(8,128)(2,1)S(1)} %bitcast.228, bf16[3,512,512]{2,1,0:T(8,128)(2,1)S(1)} %pad_maximum_fusion.1, s32[]{:T(128)S(6)} %select_n.54, bf16[8,1,512,512]{3,2,1,0:T(8,128)(2,1)} %param.7), kind=kOutput, calls=%fused_computation.47 | convolution fusion | flops 537657344 | bytes 2097156 | tf_op jit(solution)/shard_map/dot_general | solution.py:96
  113.8 2.7 %fusion.12 = bf16[8,1,512,512]{3,2,1,0:T(8,128)(2,1)} fusion(bf16[8,1,512,512]{3,2,1,0:T(8,128)(2,1)} %fusion.14, bf16[512,512]{1,0:T(8,128)(2,1)S(1)} %bitcast.229, bf16[3,512,512]{2,1,0:T(8,128)(2,1)S(1)} %pad_maximum_fusion.1, s32[]{:T(128)S(6)} %select_n.55, bf16[8,1,512,512]{3,2,1,0:T(8,128)(2,1)} %param.7), kind=kOutput, calls=%fused_computation.45 | convolution fusion | flops 537657344 | bytes 2097156 | tf_op jit(solution)/shard_map/dot_general | solution.py:96
  116.5 2.7 %fusion.10 = bf16[8,1,512,512]{3,2,1,0:T(8,128)(2,1)} fusion(bf16[8,1,512,512]{3,2,1,0:T(8,128)(2,1)} %fusion.12, bf16[512,512]{1,0:T(8,128)(2,1)S(1)} %bitcast.230, bf16[3,512,512]{2,1,0:T(8,128)(2,1)S(1)} %pad_maximum_fusion.1, s32[]{:T(128)S(6)} %select_n.56, bf16[8,1,512,512]{3,2,1,0:T(8,128)(2,1)} %param.7), kind=kOutput, calls=%fused_computation.43 | convolution fusion | flops 537657344 | bytes 2097156 | tf_op jit(solution)/shard_map/dot_general | solution.py:96
  (2 shorter events, 0.0 us)
Async XLA Ops:
  2.6 17.4 %collective-permute-start.1 = (bf16[1,512,512]{2,1,0:T(8,128)(2,1)S(1)}, bf16[1,512,512]{2,1,0:T(8,128)(2,1)S(1)}, u32[]{:S(2)}, u32[]{:S(2)}) collective-permute-start(bf16[1,512,512]{2,1,0:T(8,128)(2,1)S(1)} %broadcast_select_fusion), channel_id=1, source_target_pairs={{32,0},{64,32},{96,64},{128,96},{160,128},{192,160},{224,192},{33,... | collective-permute-start | bytes 1572872 | tf_op jit(solution)/shard_map/ppermute | solution.py:17
  4.6 16.7 %collective-permute-start = (bf16[1,512,512]{2,1,0:T(8,128)(2,1)S(1)}, bf16[1,512,512]{2,1,0:T(8,128)(2,1)S(1)}, u32[]{:S(2)}, u32[]{:S(2)}) collective-permute-start(bf16[1,512,512]{2,1,0:T(8,128)(2,1)S(1)} %broadcast_select_fusion), channel_id=1, source_target_pairs={{0,32},{32,64},{64,96},{96,128},{128,160},{160,192},{192,224},{1,3... | collective-permute-start | bytes 1572872 | tf_op jit(solution)/shard_map/ppermute | solution.py:16
  44.1 19.1 %all-to-all-start = ((bf16[32,1,16,512]{3,2,1,0:T(8,128)(2,1)}), bf16[32,1,16,512]{3,2,1,0:T(8,128)(2,1)S(1)}, u32[]{:S(2)}, u32[]{:S(2)}) async-start(bf16[32,1,16,512]{3,2,1,0:T(8,128)(2,1)} %bitcast.43), calls=%async_computation | async-start | bytes 1048576 | tf_op jit(solution)/shard_map/all_to_all | solution.py:30
  63.3 39.8 %copy-start = (bf16[1,16,512]{2,1,0:T(8,128)(2,1)}, bf16[1,16,512]{2,1,0:T(8,128)(2,1)S(1)}, u32[]{:S(2)}) copy-start(bf16[1,16,512]{2,1,0:T(8,128)(2,1)S(1)} %fusion.173) | copy-start | bytes 49156
  78.6 15.8 %collective-permute-start.3 = (bf16[1,512,512]{2,1,0:T(8,128)(2,1)S(1)}, bf16[1,512,512]{2,1,0:T(8,128)(2,1)S(1)}, u32[]{:S(2)}, u32[]{:S(2)}) collective-permute-start(bf16[1,512,512]{2,1,0:T(8,128)(2,1)S(1)} %bitcast.220), channel_id=1, source_target_pairs={{32,0},{64,32},{96,64},{128,96},{160,128},{192,160},{224,192},{33,... | collective-permute-start | bytes 1572872 | tf_op jit(solution)/shard_map/ppermute | solution.py:17
  80.5 17.0 %collective-permute-start.2 = (bf16[1,512,512]{2,1,0:T(8,128)(2,1)S(1)}, bf16[1,512,512]{2,1,0:T(8,128)(2,1)S(1)}, u32[]{:S(2)}, u32[]{:S(2)}) collective-permute-start(bf16[1,512,512]{2,1,0:T(8,128)(2,1)S(1)} %bitcast.221), channel_id=1, source_target_pairs={{0,32},{32,64},{64,96},{96,128},{128,160},{160,192},{192,224},{1,3... | collective-permute-start | bytes 1572872 | tf_op jit(solution)/shard_map/ppermute | solution.py:16
where the time goes:
time: 120 us; the launch traced here: 119 us
  matrix products  44.1 us (37%)
  waiting for transfers between devices  25.1 us (21%)
  starting transfers between devices  19.2 us (16%)
  blocking collectives  15.2 us (13%)
  between operations  11.9 us (10%)
  other arithmetic  1.91 us (2%)
  local copies, waits for them, and re-layouts  1.68 us (1%)
    dot_general x8, matrix products, padded_term(): lax.dot_general(halfway, right, (((1,), (1,)), ((), ())), preferred_eleme...  22.6 us
    dot_general x8, matrix products, shards(): lax.dot_general(update[sector], pulled, (((0,), (0,)), ((), ())), preferr...  21.5 us
    all_to_all x1, blocking collectives, from_everyone(): lax.all_to_all(jnp.broadcast_to(shard[None], (count, *shard.shape)), axis...  15.2 us
    all_to_all x1, waiting for transfers between devices, sent_and_summed(): lax.all_to_all(tiles, axis, split_axis=0, concat_axis=0, tiled=True)  10.9 us
    ppermute x2, waiting for transfers between devices, padded_2(): after = lax.ppermute(initial, axis, down)  9.75 us
    ppermute x2, starting transfers between devices, padded_2(): before = lax.ppermute(last, axis, up)  7.93 us
    all_to_all x1, starting transfers between devices, sent_and_summed(): lax.all_to_all(tiles, axis, split_axis=0, concat_axis=0, tiled=True)  7.32 us
    ppermute x2, waiting for transfers between devices, padded_2(): before = lax.ppermute(last, axis, up)  4.47 us
  transfers between devices with their start and end apart: 5, of which 4 were waited for; matrix products, arithmetic and copies ran while one was open for 2% of the time, Pallas kernels for 0%

commit v1 on v0

v1 whole, which is shorter than its diff:
```python
import functools

import jax
import jax.numpy as jnp
from jax import lax
from jax.experimental import pallas as pl
from jax.experimental.pallas import tpu as pltpu
from jax.sharding import PartitionSpec as P

MESH = pl.DeviceIdType.MESH
BF16 = jnp.bfloat16
F32 = jnp.float32
NT = (((1,), (1,)), ((), ()))
TN = (((0,), (0,)), ((), ()))
SIDE = 4
CHIPS = SIDE * SIDE
ROWS = 16


def ring_distance(step):
    return min(step, SIDE - step)


OFFSETS = sorted(
    [(dy, dx) for dy in range(SIDE) for dx in range(SIDE) if (dy, dx) != (0, 0)],
    key=lambda o: -(ring_distance(o[0]) + ring_distance(o[1])),
)


def product_kernel(
    shifts, widths, steps, state_hbm, left_hbm, right_hbm,
    upd_out, w_out,
    state, ext0, ext1, left, right, half, total, sibout, sibin, sums, arrived, upd,
    load_sem, left_sem, right_sem, out_sem,
    z1_send, z1_recv, f1_send, f1_recv, sib_send, sib_recv,
    rs_send, rs_recv, ag_send, ag_recv, agf_send, agf_recv,
    z2_send, z2_recv, z2f_send, z2f_recv,
):
    ext = (ext0, ext1)
    sectors = lax.axis_size("sec")
    z = lax.axis_index("sec")
    chan = lax.axis_index("chan")
    core = lax.rem(chan, 2)
    chip = chan // 2
    y, x = chip // SIDE, lax.rem(chip, SIDE)
    sib = chan + 1 - 2 * core
    channels = left_hbm.shape[0]
    pad = state_hbm.shape[1]
    wide = pad // 2

    load = pltpu.make_async_copy(state_hbm.at[0], state, load_sem)
    load.start()
    loads = []
    for c in range(channels):
        copy = pltpu.make_async_copy(left_hbm.at[c, 0], left.at[c], left_sem.at[c])
        copy.start()
        loads.append(copy)
    for j in range(2):
        for c in range(channels):
            copy = pltpu.make_async_copy(
                right_hbm.at[c, 0, :, pl.ds(j * wide, wide)],
                right.at[j, :, pl.ds(c * wide, wide)],
                right_sem.at[j, c],
            )
            copy.start()
            loads.append(copy)

    def peer(dy, dx):
        there = lax.rem(y + dy, SIDE) * SIDE + lax.rem(x + dx, SIDE)
        return there

    barrier = pltpu.get_barrier_semaphore()
    up, down = lax.rem(z + 1, sectors), lax.rem(z + sectors - 1, sectors)
    for target in (up, down):
        pl.semaphore_signal(barrier, 1, device_id=(target, chan), device_id_type=MESH)
    pl.semaphore_signal(barrier, 1, device_id=(z, sib), device_id_type=MESH)
    for dy, dx in OFFSETS:
        pl.semaphore_signal(
            barrier, 1, device_id=(z, peer(dy, dx) * 2 + core), device_id_type=MESH
        )

    load.wait()
    width = widths[0]
    rows_at = lax.broadcasted_iota(jnp.int32, (pad, pad), 0)
    cols_at = lax.broadcasted_iota(jnp.int32, (pad, pad), 1)
    kept = jnp.where((rows_at < width) & (cols_at < width), state[...].astype(F32), 0.0).astype(BF16)
    ext0[1] = kept[:, :wide]
    ext1[1] = kept[:, wide:]

    @pl.when(z == 0)
    def _():
        ext0[0] = jnp.zeros((pad, wide), BF16)
        ext1[0] = jnp.zeros((pad, wide), BF16)
        upd[0] = jnp.zeros((pad, pad), BF16)

    @pl.when(z == sectors - 1)
    def _():
        ext0[2] = jnp.zeros((pad, wide), BF16)
        ext1[2] = jnp.zeros((pad, wide), BF16)
        upd[2] = jnp.zeros((pad, pad), BF16)

    pl.semaphore_wait(barrier, 3 + len(OFFSETS))

    slots = (0, 2)
    can_send = (z < sectors - 1, z > 0)
    can_take = (z > 0, z < sectors - 1)
    targets = (up, down)
    part = pl.ds(pl.multiple_of(core * (wide // 2), wide // 2), wide // 2)
    other = pl.ds(pl.multiple_of((1 - core) * (wide // 2), wide // 2), wide // 2)

    def halo(j, d):
        return pltpu.make_async_remote_copy(
            ext[j].at[1, :, part], ext[j].at[slots[d], :, part],
            z1_send.at[j, d], z1_recv.at[j, d],
            device_id=(targets[d], chan), device_id_type=MESH,
        )

    def handed(j, d, columns):
        return pltpu.make_async_remote_copy(
            ext[j].at[slots[d], :, columns], ext[j].at[slots[d], :, columns],
            f1_send.at[j, d], f1_recv.at[j, d],
            device_id=(z, sib), device_id_type=MESH,
        )

    for j in range(2):
        for d in range(2):
            @pl.when(can_send[d])
            def _():
                halo(j, d).start()
    for copy in loads:
        copy.wait()
    for j in range(2):
        for d in range(2):
            @pl.when(can_take[d])
            def _():
                halo(j, d).wait_recv()
                handed(j, d, part).start()
        for d in range(2):
            @pl.when(can_take[d])
            def _():
                handed(j, d, other).wait_recv()
        for c in range(channels):
            source = ext[j][1 - shifts[c]]
            half[:, pl.ds(c * wide, wide)] = jnp.dot(
                left[c], source, preferred_element_type=F32
            ).astype(BF16)
        for r in range(2):
            value = lax.dot_general(
                half[pl.ds(r * wide, wide), :], right[j], NT, preferred_element_type=F32
            ).reshape(CHIPS // 2, 2, ROWS, pad)
            here = pl.ds(r * CHIPS // 2, CHIPS // 2)
            if j == 0:
                total[here] = value
            else:
                total[here] = total[here] + value
                sibout[here] = total[here, 1 - core].astype(BF16)
                pltpu.make_async_remote_copy(
                    sibout.at[here], sibin.at[here], sib_send.at[r], sib_recv.at[r],
                    device_id=(z, sib), device_id_type=MESH,
                ).start()

    for r in range(2):
        here = pl.ds(r * CHIPS // 2, CHIPS // 2)
        pltpu.make_async_remote_copy(
            sibout.at[here], sibin.at[here], sib_send.at[r], sib_recv.at[r],
            device_id=(z, sib), device_id_type=MESH,
        ).wait()
        pair = total[here, core] + sibin[here].astype(F32)
        sums[here] = pair.astype(BF16)
        total[here, core] = pair

    def scattered(i):
        dy, dx = OFFSETS[i]
        there = peer(dy, dx)
        return pltpu.make_async_remote_copy(
            sums.at[there], arrived.at[i], rs_send.at[i], rs_recv.at[i],
            device_id=(z, there * 2 + core), device_id_type=MESH,
        )

    for i in range(len(OFFSETS)):
        scattered(i).start()
    acc = total[chip, core]
    for i in reversed(range(len(OFFSETS))):
        scattered(i).wait_recv()
        acc = acc + arrived[i].astype(F32)

    first = pl.multiple_of(chan * ROWS, ROWS)
    mine = pl.ds(first, ROWS)
    row_ids = first + lax.broadcasted_iota(jnp.int32, (ROWS, pad), 0)
    col_ids = lax.broadcasted_iota(jnp.int32, (ROWS, pad), 1)
    before = jnp.concatenate([ext0[1, mine, :], ext1[1, mine, :]], axis=1).astype(F32)
    corrected = jnp.where((row_ids < width) & (col_ids < width), before - steps[0] * acc, 0.0)
    upd[1, mine, :] = corrected.astype(BF16)

    def rows_of(where, parity):
        return pl.ds(pl.multiple_of((where * 2 + parity) * ROWS, ROWS), ROWS)

    def origin(i):
        if i == len(OFFSETS):
            return chip
        dy, dx = OFFSETS[i]
        return peer(SIDE - dy, SIDE - dx)

    def gathered(i, where):
        dy, dx = OFFSETS[i]
        rows = rows_of(where, core)
        return pltpu.make_async_remote_copy(
            upd.at[1, rows], upd.at[1, rows], ag_send.at[i], ag_recv.at[i],
            device_id=(z, peer(dy, dx) * 2 + core), device_id_type=MESH,
        )

    def to_sibling(i, parity):
        rows = rows_of(origin(i), parity)
        return pltpu.make_async_remote_copy(
            upd.at[1, rows], upd.at[1, rows], agf_send.at[i], agf_recv.at[i],
            device_id=(z, sib), device_id_type=MESH,
        )

    def over_z(i, d):
        rows = rows_of(origin(i), core)
        return pltpu.make_async_remote_copy(
            upd.at[1, rows], upd.at[slots[d], rows], z2_send.at[d, i], z2_recv.at[d, i],
            device_id=(targets[d], chan), device_id_type=MESH,
        )

    def pass_on(i):
        to_sibling(i, core).start()
        for d in range(2):
            @pl.when(can_send[d])
            def _():
                over_z(i, d).start()

    for i in range(len(OFFSETS)):
        gathered(i, chip).start()
    pass_on(len(OFFSETS))
    for i in reversed(range(len(OFFSETS))):
        gathered(i, origin(i)).wait_recv()
        pass_on(i)
    for i in range(len(OFFSETS) + 1):
        to_sibling(i, 1 - core).wait_recv()

    turned = upd[1].T
    outs = []
    for c in range(channels):
        left[c] = jnp.dot(turned, left[c], preferred_element_type=F32).astype(BF16)
        copy = pltpu.make_async_copy(left.at[c], w_out.at[c], out_sem.at[c])
        copy.start()
        outs.append(copy)
    own = pltpu.make_async_copy(upd.at[1], upd_out.at[1], out_sem.at[channels])
    own.start()
    outs.append(own)

    def halo_handed(i, d, parity):
        rows = rows_of(origin(i), parity)
        return pltpu.make_async_remote_copy(
            upd.at[slots[d], rows], upd.at[slots[d], rows], z2f_send.at[d, i], z2f_recv.at[d, i],
            device_id=(z, sib), device_id_type=MESH,
        )

    order = [len(OFFSETS)] + list(reversed(range(len(OFFSETS))))
    for i in order:
        for d in range(2):
            @pl.when(can_take[d])
            def _():
                over_z(i, d).wait_recv()
                halo_handed(i, d, core).start()
    for i in order:
        for d in range(2):
            @pl.when(can_take[d])
            def _():
                halo_handed(i, d, 1 - core).wait_recv()
    for d in range(2):
        copy = pltpu.make_async_copy(
            upd.at[slots[d]], upd_out.at[slots[d]], out_sem.at[channels + 1 + d]
        )
        copy.start()
        outs.append(copy)

    for j in range(2):
        for d in range(2):
            @pl.when(can_send[d])
            def _():
                halo(j, d).wait_send()

            @pl.when(can_take[d])
            def _():
                handed(j, d, part).wait_send()
    for i in range(len(OFFSETS)):
        scattered(i).wait_send()
        gathered(i, chip).wait_send()
    for i in range(len(OFFSETS) + 1):
        to_sibling(i, core).wait_send()
        for d in range(2):
            @pl.when(can_send[d])
            def _():
                over_z(i, d).wait_send()

            @pl.when(can_take[d])
            def _():
                halo_handed(i, d, core).wait_send()
    for copy in outs:
        copy.wait()


def rotate_kernel(shifts, first, scale, w_ref, upd_ref, rows_ref, out_ref):
    channel = pl.program_id(0)
    source = upd_ref[1 - shifts[channel]]
    out_ref[0, 0] = (jnp.dot(w_ref[0], source, preferred_element_type=F32) * scale).astype(BF16)

    @pl.when(channel == 0)
    def _():
        rows_ref[0] = upd_ref[1, pl.ds(pl.multiple_of(first[0], ROWS), ROWS), :]


def shards(state_blocks, left_blocks, right_blocks, widths, step_sizes, shifts):
    channels, _, pad, _ = left_blocks.shape
    wide = pad // 2
    n = len(OFFSETS)
    smem = pl.BlockSpec(memory_space=pltpu.SMEM)
    hbm = pl.BlockSpec(memory_space=pl.ANY)
    dma = pltpu.SemaphoreType.DMA
    upd, turned = pl.pallas_call(
        product_kernel,
        name="product",
        out_shape=(
            jax.ShapeDtypeStruct((3, pad, pad), BF16),
            jax.ShapeDtypeStruct((channels, pad, pad), BF16),
        ),
        in_specs=[smem] * 3 + [hbm] * 3,
        out_specs=(hbm, hbm),
        scratch_shapes=[
            pltpu.VMEM((pad, pad), BF16),
            pltpu.VMEM((3, pad, wide), BF16),
            pltpu.VMEM((3, pad, wide), BF16),
            pltpu.VMEM((channels, pad, pad), BF16),
            pltpu.VMEM((2, pad, channels * wide), BF16),
            pltpu.VMEM((pad, channels * wide), BF16),
            pltpu.VMEM((CHIPS, 2, ROWS, pad), F32),
            pltpu.VMEM((CHIPS, ROWS, pad), BF16),
            pltpu.VMEM((CHIPS, ROWS, pad), BF16),
            pltpu.VMEM((CHIPS, ROWS, pad), BF16),
            pltpu.VMEM((n, ROWS, pad), BF16),
            pltpu.VMEM((3, pad, pad), BF16),
            dma(()), dma((channels,)), dma((2, channels)), dma((channels + 3,)),
            dma((2, 2)), dma((2, 2)), dma((2, 2)), dma((2, 2)), dma((2,)), dma((2,)),
            dma((n,)), dma((n,)), dma((n,)), dma((n,)), dma((n + 1,)), dma((n + 1,)),
            dma((2, n + 1)), dma((2, n + 1)), dma((2, n + 1)), dma((2, n + 1)),
        ],
        compiler_params=pltpu.CompilerParams(
            collective_id=0, has_side_effects=True, vmem_limit_bytes=32 << 20
        ),
        cost_estimate=pl.CostEstimate(flops=6 << 30, bytes_accessed=16 << 20, transcendentals=0),
    )(shifts, widths, step_sizes, state_blocks, left_blocks, right_blocks)

    first = (lax.axis_index("chan") * ROWS).astype(jnp.int32).reshape(1)
    rows, new_left = pl.pallas_call(
        lambda s, f, *refs: rotate_kernel(s, f, pad ** (-0.5), *refs),
        name="rotate",
        out_shape=(
            jax.ShapeDtypeStruct((1, ROWS, pad), BF16),
            jax.ShapeDtypeStruct((channels, 1, pad, pad), BF16),
        ),
        grid_spec=pltpu.PrefetchScalarGridSpec(
            num_scalar_prefetch=2,
            grid=(channels,),
            in_specs=[
                pl.BlockSpec((1, pad, pad), lambda c, s, f: (c, 0, 0)),
                pl.BlockSpec((3, pad, pad), lambda c, s, f: (0, 0, 0)),
            ],
            out_specs=(
                pl.BlockSpec((1, ROWS, pad), lambda c, s, f: (0, 0, 0)),
                pl.BlockSpec((1, 1, pad, pad), lambda c, s, f: (c, 0, 0, 0)),
            ),
        ),
        compiler_params=pltpu.CompilerParams(vmem_limit_bytes=16 << 20),
        cost_estimate=pl.CostEstimate(flops=2 << 30, bytes_accessed=10 << 20, transcendentals=0),
    )(shifts, first, turned, upd)
    return rows, new_left


def solution(mesh):
    placed = (
        P("sec", None, None),
        P("chan", "sec", None, None),
        P("chan", "sec", None, None),
        P("sec"),
        P("sec"),
        P("chan"),
    )
    return jax.shard_map(
        shards,
        mesh=mesh,
        in_specs=placed,
        out_specs=(P("sec", "chan", None), P("chan", "sec", None, None)),
        check_vma=False,
    )
```

time: 120 us -> 59.8 us (0.50)
  the two profiles are of different devices: /device:TPU:128 before, /device:TPU:1 now
where the time goes in v1:
time: 59.8 us; the launch traced here: 59.5 us
  Pallas kernels  51.5 us (86%)
  local copies, waits for them, and re-layouts  6.06 us (10%)
  between operations  1.94 us (3%)
    pallas_call x1, Pallas kernels, shards(): pl.pallas_call(product_kernel, name='product', out_shape=(jax.ShapeDtypeS...  45.6 us
    unnamed x8, local copies, waits for them, and re-layouts  6.06 us
    pallas_call x1, Pallas kernels, shards(): pl.pallas_call(lambda s, f, *refs: rotate_kernel(s, f, pad ** (-0.5), *re...  5.96 us

profile of v1, /device:TPU:1, one launch (start us, length us, event | category | flops | bytes accessed | tf_op | source)
XLA Modules:
  0.0 59.5 jit_solution(10818127410806728564)
XLA Ops:
  1.9 0.0 copy-start
  1.9 2.2 %copy-done = bf16[8,1,512,512]{3,2,1,0:T(8,128)(2,1)S(1)} copy-done((bf16[8,1,512,512]{3,2,1,0:T(8,128)(2,1)S(1)}, bf16[8,1,512,512]{3,2,1,0:T(8,128)(2,1)}, u32[]{:S(2)}) %copy-start) | copy-done | bytes 4194328
  4.1 0.0 copy-start.1
  4.1 2.2 %copy-done.1 = bf16[8,1,512,512]{3,2,1,0:T(8,128)(2,1)S(1)} copy-done((bf16[8,1,512,512]{3,2,1,0:T(8,128)(2,1)S(1)}, bf16[8,1,512,512]{3,2,1,0:T(8,128)(2,1)}, u32[]{:S(2)}) %copy-start.1) | copy-done | bytes 4194328
  6.3 0.0 copy-start.2
  6.3 1.0 %copy-done.2 = bf16[1,512,512]{2,1,0:T(8,128)(2,1)S(1)} copy-done((bf16[1,512,512]{2,1,0:T(8,128)(2,1)S(1)}, bf16[1,512,512]{2,1,0:T(8,128)(2,1)}, u32[]{:S(2)}) %copy-start.2) | copy-done | bytes 524312
  7.3 0.0 copy-start.3
  7.3 0.7 %copy-done.3 = s32[8]{0:T(128)S(1)} copy-done((s32[8]{0:T(128)S(1)}, s32[8]{0:T(128)}, u32[]{:S(2)}) %copy-start.3) | copy-done | bytes 56
  8.0 45.6 %product.1 = (bf16[3,512,512]{2,1,0:T(8,128)(2,1)S(1)}, bf16[8,512,512]{2,1,0:T(8,128)(2,1)S(1)}) custom-call(s32[8]{0:T(128)S(1)} %copy-done.3, s32[1]{0:T(128)S(6)} %copy.8.widths, f32[1]{0:T(128)S(6)} %copy.9.steps, bf16[1,512,512]{2,1,0:T(8,128)(2,1)S(1)} %copy-done.2, bf16[8,1,512,512]{3,2,1,0:T(8,128)(2,1)S(1)} %copy-done, ...), custom_call_target="tpu_custom_call" | custom-call | flops 6442450944 | bytes 16777216 | tf_op jit(solution)/shard_map/product/pallas_call | solution.py:322
  53.6 6.0 %rotate.1 = (bf16[1,16,512]{2,1,0:T(8,128)(2,1)}, bf16[8,1,512,512]{3,2,1,0:T(8,128)(2,1)}) custom-call(s32[8]{0:T(128)S(1)} %copy-done.3, s32[1]{0:T(128)} %bitcast.f, bf16[8,512,512]{2,1,0:T(8,128)(2,1)S(1)} %get-tuple-element.4.refs_0_, bf16[3,512,512]{2,1,0:T(8,128)(2,1)S(1)} %get-tuple-element.5.refs_1_), custom_call_target="tpu_custom_call" | custom-call | flops 2147483648 | bytes 10485760 | tf_op jit(solution)/shard_map/rotate/pallas_call | solution.py:356
Async XLA Ops:
  1.9 2.2 %copy-start = (bf16[8,1,512,512]{3,2,1,0:T(8,128)(2,1)S(1)}, bf16[8,1,512,512]{3,2,1,0:T(8,128)(2,1)}, u32[]{:S(2)}) copy-start(bf16[8,1,512,512]{3,2,1,0:T(8,128)(2,1)} %left_hbm.1) | copy-start | bytes 12582916
  4.1 2.2 %copy-start.1 = (bf16[8,1,512,512]{3,2,1,0:T(8,128)(2,1)S(1)}, bf16[8,1,512,512]{3,2,1,0:T(8,128)(2,1)}, u32[]{:S(2)}) copy-start(bf16[8,1,512,512]{3,2,1,0:T(8,128)(2,1)} %right_hbm.1) | copy-start | bytes 12582916
  6.3 1.0 %copy-start.2 = (bf16[1,512,512]{2,1,0:T(8,128)(2,1)S(1)}, bf16[1,512,512]{2,1,0:T(8,128)(2,1)}, u32[]{:S(2)}) copy-start(bf16[1,512,512]{2,1,0:T(8,128)(2,1)} %state_hbm.1) | copy-start | bytes 1572868
  7.3 0.7 %copy-start.3 = (s32[8]{0:T(128)S(1)}, s32[8]{0:T(128)}, u32[]{:S(2)}) copy-start(s32[8]{0:T(128)} %s.1) | copy-start | bytes 100

commit v2 on v1

v2 whole, which is shorter than its diff:
```python
import functools

import jax
import jax.numpy as jnp
from jax import lax
from jax.experimental import pallas as pl
from jax.experimental.pallas import tpu as pltpu
from jax.sharding import PartitionSpec as P

MESH = pl.DeviceIdType.MESH
BF16 = jnp.bfloat16
F32 = jnp.float32
NT = (((1,), (1,)), ((), ()))
SIDE = 4
CHIPS = SIDE * SIDE
ROWS = 16


def ring_distance(step):
    return min(step, SIDE - step)


OFFSETS = sorted(
    [(dy, dx) for dy in range(SIDE) for dx in range(SIDE) if (dy, dx) != (0, 0)],
    key=lambda o: -(ring_distance(o[0]) + ring_distance(o[1])),
)


GROUPS = [(0, 0), (0, 1), (0, 3), (0, 2), (1, None), (3, None), (2, None)]


def product_kernel(
    shifts, widths, steps, state_hbm, left_hbm, right_hbm,
    upd, w_out,
    state, ext0, ext1, left, right, half, total, sibout, sibin, sums, arrived,
    load_sem, z1_send, z1_recv, f1_send, f1_recv, sib_send, sib_recv,
    rs_send, rs_recv, ag_send, ag_recv, agf_send, agf_recv,
    z2_send, z2_recv, z2f_send, z2f_recv,
):
    ext = (ext0, ext1)
    sectors = lax.axis_size("sec")
    z = lax.axis_index("sec")
    chan = lax.axis_index("chan")
    core = lax.rem(chan, 2)
    chip = chan // 2
    y, x = chip // SIDE, lax.rem(chip, SIDE)
    sib = chan + 1 - 2 * core
    channels = left_hbm.shape[0]
    pad = state_hbm.shape[1]
    wide = pad // 2
    up, down = lax.rem(z + 1, sectors), lax.rem(z + sectors - 1, sectors)

    def peer(dy, dx):
        return lax.rem(y + dy, SIDE) * SIDE + lax.rem(x + dx, SIDE)

    def remote(src, dst, send, recv, where, there):
        return pltpu.make_async_remote_copy(
            src, dst, send, recv, device_id=(where, there), device_id_type=MESH
        )

    def wait_bytes(ref, sem):
        pltpu.make_async_copy(ref, ref, sem).wait()

    load = pltpu.make_async_copy(state_hbm.at[0], state, load_sem.at[0])
    load.start()
    barrier = pltpu.get_barrier_semaphore()
    for target in (up, down):
        pl.semaphore_signal(barrier, 1, device_id=(target, chan), device_id_type=MESH)
    for dy, dx in OFFSETS:
        pl.semaphore_signal(
            barrier, 1, device_id=(z, peer(dy, dx) * 2 + core), device_id_type=MESH
        )
    pl.semaphore_signal(barrier, 1, device_id=(z, sib), device_id_type=MESH)

    load.wait()
    width = widths[0]
    rows_at = lax.broadcasted_iota(jnp.int32, (pad, wide), 0)
    cols_at = lax.broadcasted_iota(jnp.int32, (pad, wide), 1)
    for j in range(2):
        kept = (rows_at < width) & (cols_at < width - j * wide)
        values = state[:, pl.ds(j * wide, wide)].astype(F32)
        ext[j][1] = jnp.where(kept, values, 0.0).astype(BF16)

    slots = (0, 2)
    can_send = (z < sectors - 1, z > 0)
    can_take = (z > 0, z < sectors - 1)
    targets = (up, down)
    part = pl.ds(pl.multiple_of(core * wide, wide), wide)
    other = pl.ds(pl.multiple_of((1 - core) * wide, wide), wide)

    def halo(j, d):
        return remote(
            ext[j].at[1, part], ext[j].at[slots[d], part],
            z1_send.at[j, d], z1_recv.at[j, d], targets[d], chan,
        )

    def handed(j, d, rows):
        return remote(
            ext[j].at[slots[d], rows], ext[j].at[slots[d], rows],
            f1_send.at[j, d], f1_recv.at[j, d], z, sib,
        )

    pl.semaphore_wait(barrier, 3 + len(OFFSETS))
    for j in range(2):
        for d in range(2):
            pl.when(can_send[d])(halo(j, d).start)
    loads = [pltpu.make_async_copy(left_hbm.at[:, 0], left, load_sem.at[1])]
    for j in range(2):
        loads.append(
            pltpu.make_async_copy(
                right_hbm.at[:, 0, :, pl.ds(j * wide, wide)], right.at[j], load_sem.at[2 + j]
            )
        )
    for copy in loads:
        copy.start()

    @pl.when(z == 0)
    def _():
        ext0[0] = jnp.zeros((pad, wide), BF16)
        ext1[0] = jnp.zeros((pad, wide), BF16)
        upd[0] = jnp.zeros(upd.shape[1:], BF16)

    @pl.when(z == sectors - 1)
    def _():
        ext0[2] = jnp.zeros((pad, wide), BF16)
        ext1[2] = jnp.zeros((pad, wide), BF16)
        upd[2] = jnp.zeros(upd.shape[1:], BF16)

    for copy in loads:
        copy.wait()

    def hand_over(j):
        for d in range(2):
            @pl.when(can_take[d])
            def _():
                halo(j, d).wait_recv()
                handed(j, d, part).start()

    def pair_sent(r):
        here = pl.ds(r * CHIPS // 2, CHIPS // 2)
        return remote(sibout.at[here], sibin.at[here], sib_send.at[r], sib_recv.at[r], z, sib)

    hand_over(0)
    for j in range(2):
        for d in range(2):
            pl.when(can_take[d])(handed(j, d, other).wait_recv)
        for c in range(channels):
            source = ext[j][1 - shifts[c]]
            half[:, pl.ds(c * wide, wide)] = jnp.dot(
                left[c], source, preferred_element_type=F32
            ).astype(BF16)
        for r in range(2):
            beside = jnp.concatenate([right[j, c] for c in range(channels)], axis=1)
            value = lax.dot_general(
                half[pl.ds(r * wide, wide), :], beside, NT, preferred_element_type=F32
            ).reshape(CHIPS // 2, 2, ROWS, pad)
            here = pl.ds(r * CHIPS // 2, CHIPS // 2)
            if j == 0:
                total[here] = value
                if r == 0:
                    hand_over(1)
            else:
                total[here] = total[here] + value
                sibout[here] = total[here, 1 - core].astype(BF16)
                pair_sent(r).start()

    for r in range(2):
        here = pl.ds(r * CHIPS // 2, CHIPS // 2)
        pair_sent(r).wait_recv()
        pair = total[here, core] + sibin[here].astype(F32)
        sums[here] = pair.astype(BF16)
        total[here, core] = pair
    for i, (dy, dx) in enumerate(OFFSETS):
        there = peer(dy, dx)
        remote(sums.at[there], arrived.at[i], rs_send, rs_recv, z, there * 2 + core).start()

    for j in range(2):
        for d in range(2):
            pl.when(can_send[d])(halo(j, d).wait_send)
            pl.when(can_take[d])(handed(j, d, part).wait_send)
        pair_sent(j).wait_send()

    first = pl.multiple_of(chan * ROWS, ROWS)
    mine = pl.ds(first, ROWS)
    row_ids = first + lax.broadcasted_iota(jnp.int32, (ROWS, pad), 0)
    col_ids = lax.broadcasted_iota(jnp.int32, (ROWS, pad), 1)
    before = jnp.concatenate([ext0[1, mine, :], ext1[1, mine, :]], axis=1).astype(F32)
    acc = total[chip, core]
    wait_bytes(arrived, rs_recv)
    for i in range(len(OFFSETS)):
        acc = acc + arrived[i].astype(F32)
    corrected = jnp.where((row_ids < width) & (col_ids < width), before - steps[0] * acc, 0.0)
    upd[1, chip, core] = corrected.astype(BF16)

    def group(slot, g, parity):
        gy, gx = GROUPS[g]
        if gx is None:
            rows = pl.ds(pl.multiple_of(lax.rem(y + gy, SIDE) * SIDE, SIDE), SIDE)
            return upd.at[slot, rows, parity]
        return upd.at[slot, peer(gy, gx), parity]

    def gathered(i, where):
        dy, dx = OFFSETS[i]
        block = upd.at[1, where, core]
        return remote(block, block, ag_send, ag_recv.at[i], z, peer(dy, dx) * 2 + core)

    def take(gy, gx):
        i = OFFSETS.index(((SIDE - gy) % SIDE, (SIDE - gx) % SIDE))
        gathered(i, peer(gy, gx)).wait_recv()

    def to_sibling(g, parity):
        block = group(1, g, parity)
        return remote(block, block, agf_send.at[g], agf_recv.at[g], z, sib)

    def over_z(g, d):
        return remote(
            group(1, g, core), group(slots[d], g, core),
            z2_send.at[d, g], z2_recv.at[d, g], targets[d], chan,
        )

    def z_on(g):
        for d in range(2):
            pl.when(can_send[d])(over_z(g, d).start)

    z_on(0)
    for i in range(len(OFFSETS)):
        gathered(i, chip).start()
    to_sibling(0, core).start()
    for g in range(1, len(GROUPS)):
        gy, gx = GROUPS[g]
        for taken in range(SIDE) if gx is None else (gx,):
            take(gy, taken)
        z_on(g)
        to_sibling(g, core).start()
    wait_bytes(arrived, rs_send)
    wait_bytes(arrived, ag_send)
    for g in range(len(GROUPS)):
        to_sibling(g, 1 - core).wait_recv()

    def halo_handed(gy, d, parity):
        rows = pl.ds(pl.multiple_of(lax.rem(y + gy, SIDE) * SIDE, SIDE), SIDE)
        block = upd.at[slots[d], rows, parity]
        return remote(block, block, z2f_send.at[d, gy], z2f_recv.at[d, gy], z, sib)

    def hand_row(gy):
        for d in range(2):
            @pl.when(can_take[d])
            def _():
                for g in range(len(GROUPS)):
                    if GROUPS[g][0] == gy:
                        over_z(g, d).wait_recv()
                halo_handed(gy, d, core).start()

    hand_row(0)
    turned = upd[1].reshape(pad, pad).T
    for c in range(channels):
        if c == channels // 2:
            hand_row(1)
            hand_row(3)
        w_out[c] = jnp.dot(turned, left[c], preferred_element_type=F32).astype(BF16)
    hand_row(2)
    for g in range(len(GROUPS)):
        to_sibling(g, core).wait_send()
        for d in range(2):
            pl.when(can_send[d])(over_z(g, d).wait_send)
    for gy in range(SIDE):
        for d in range(2):
            @pl.when(can_take[d])
            def _():
                halo_handed(gy, d, core).wait_send()
                halo_handed(gy, d, 1 - core).wait_recv()


def rotate_kernel(scale, shifts, w, upd, rows_out, out, done, sem):
    channels, pad, _ = w.shape
    chan = lax.axis_index("chan")
    rows = pltpu.make_async_copy(
        upd.at[1, chan // 2, lax.rem(chan, 2)], rows_out.at[0], sem.at[channels]
    )
    rows.start()
    copies = [pltpu.make_async_copy(done.at[c], out.at[c, 0], sem.at[c]) for c in range(channels)]
    for c in range(channels):
        source = upd[1 - shifts[c]].reshape(pad, pad)
        done[c] = (jnp.dot(w[c], source, preferred_element_type=F32) * scale).astype(BF16)
        copies[c].start()
    rows.wait()
    for copy in copies:
        copy.wait()


def shards(state_blocks, left_blocks, right_blocks, widths, step_sizes, shifts):
    channels, _, pad, _ = left_blocks.shape
    wide = pad // 2
    n, m = len(OFFSETS), len(GROUPS)
    smem = pl.BlockSpec(memory_space=pltpu.SMEM)
    hbm = pl.BlockSpec(memory_space=pltpu.HBM)
    vmem = pl.BlockSpec(memory_space=pltpu.VMEM)
    dma = pltpu.SemaphoreType.DMA
    blocks = (pltpu.with_memory_space_constraint(a, pltpu.HBM) for a in (state_blocks, left_blocks, right_blocks))
    upd, turned = pl.pallas_call(
        product_kernel,
        name="product",
        out_shape=(
            jax.ShapeDtypeStruct((3, CHIPS, 2, ROWS, pad), BF16),
            jax.ShapeDtypeStruct((channels, pad, pad), BF16),
        ),
        in_specs=[smem] * 3 + [hbm] * 3,
        out_specs=(vmem, vmem),
        scratch_shapes=[
            pltpu.VMEM((pad, pad), BF16),
            pltpu.VMEM((3, pad, wide), BF16),
            pltpu.VMEM((3, pad, wide), BF16),
            pltpu.VMEM((channels, pad, pad), BF16),
            pltpu.VMEM((2, channels, pad, wide), BF16),
            pltpu.VMEM((pad, channels * wide), BF16),
            pltpu.VMEM((CHIPS, 2, ROWS, pad), F32),
            pltpu.VMEM((CHIPS, ROWS, pad), BF16),
            pltpu.VMEM((CHIPS, ROWS, pad), BF16),
            pltpu.VMEM((CHIPS, ROWS, pad), BF16),
            pltpu.VMEM((n, ROWS, pad), BF16),
            dma((4,)), dma((2, 2)), dma((2, 2)), dma((2, 2)), dma((2, 2)), dma((2,)), dma((2,)),
            dma(()), dma(()), dma(()), dma((n,)), dma((m,)), dma((m,)),
            dma((2, m)), dma((2, m)), dma((2, SIDE)), dma((2, SIDE)),
        ],
        compiler_params=pltpu.CompilerParams(
            collective_id=0, has_side_effects=True, vmem_limit_bytes=32 << 20
        ),
        cost_estimate=pl.CostEstimate(flops=6 << 30, bytes_accessed=16 << 20, transcendentals=0),
    )(shifts, widths, step_sizes, *blocks)

    rows, new_left = pl.pallas_call(
        functools.partial(rotate_kernel, pad ** (-0.5)),
        name="rotate",
        out_shape=(
            jax.ShapeDtypeStruct((1, ROWS, pad), BF16),
            jax.ShapeDtypeStruct((channels, 1, pad, pad), BF16),
        ),
        in_specs=[smem, vmem, vmem],
        out_specs=(hbm, hbm),
        scratch_shapes=[
            pltpu.VMEM((channels, pad, pad), BF16),
            dma((channels + 1,)),
        ],
        compiler_params=pltpu.CompilerParams(vmem_limit_bytes=16 << 20),
        cost_estimate=pl.CostEstimate(flops=2 << 30, bytes_accessed=10 << 20, transcendentals=0),
    )(shifts, turned, upd)
    return rows, new_left


def solution(mesh):
    placed = (
        P("sec", None, None),
        P("chan", "sec", None, None),
        P("chan", "sec", None, None),
        P("sec"),
        P("sec"),
        P("chan"),
    )
    return jax.shard_map(
        shards,
        mesh=mesh,
        in_specs=placed,
        out_specs=(P("sec", "chan", None), P("chan", "sec", None, None)),
        check_vma=False,
    )
```

time: 59.8 us -> 49.9 us (0.83)
  local copies, waits for them, and re-layouts: 6.06 us -> 0.65 us
  Pallas kernels: 51.5 us -> 47.2 us
    unnamed x8 -> x2, local copies, waits for them, and re-layouts: 6.06 us -> 0.65 us
    pallas_call x1, Pallas kernels: 5.96 us -> 3.77 us  [shards(): pl.pallas_call(functools.partial(rotate_kernel, pad ** (-0.5)), name='rot...]
    pallas_call x1, Pallas kernels: 45.6 us -> 43.4 us  [shards(): pl.pallas_call(product_kernel, name='product', out_shape=(jax.ShapeDtypeS...]
where the time goes in v2:
time: 49.9 us; the launch traced here: 49.8 us
  Pallas kernels  47.2 us (95%)
  between operations  1.94 us (4%)
  local copies, waits for them, and re-layouts  0.65 us (1%)
    pallas_call x1, Pallas kernels, shards(): pl.pallas_call(product_kernel, name='product', out_shape=(jax.ShapeDtypeS...  43.4 us
    pallas_call x1, Pallas kernels, shards(): pl.pallas_call(functools.partial(rotate_kernel, pad ** (-0.5)), name='rot...  3.77 us

profile of v2, /device:TPU:1, one launch (start us, length us, event | category | flops | bytes accessed | tf_op | source)
XLA Modules:
  0.0 49.8 jit_solution(2937483791748833033)
XLA Ops:
  1.9 0.0 copy-start
  1.9 0.6 %copy-done = s32[8]{0:T(128)S(1)} copy-done((s32[8]{0:T(128)S(1)}, s32[8]{0:T(128)}, u32[]{:S(2)}) %copy-start) | copy-done | bytes 56
  2.6 43.4 %product.1 = (bf16[3,16,2,16,512]{4,3,2,1,0:T(8,128)(2,1)S(1)}, bf16[8,512,512]{2,1,0:T(8,128)(2,1)S(1)}) custom-call(s32[8]{0:T(128)S(1)} %copy-done, s32[1]{0:T(128)S(6)} %copy.8.widths, f32[1]{0:T(128)S(6)} %copy.9.steps, bf16[1,512,512]{2,1,0:T(8,128)(2,1)} %state_hbm.1, bf16[8,1,512,512]{3,2,1,0:T(8,128)(2,1)} %left_hbm.1, ...), custom_call_target="tpu_custom_call" | custom-call | flops 6442450944 | bytes 16777216 | tf_op jit(solution)/shard_map/product/pallas_call | solution.py:300
  46.0 3.8 %rotate.1 = (bf16[1,16,512]{2,1,0:T(8,128)(2,1)}, bf16[8,1,512,512]{3,2,1,0:T(8,128)(2,1)}) custom-call(s32[8]{0:T(128)S(1)} %copy-done, bf16[8,512,512]{2,1,0:T(8,128)(2,1)S(1)} %get-tuple-element.4.w, bf16[3,16,2,16,512]{4,3,2,1,0:T(8,128)(2,1)S(1)} %get-tuple-element.5.upd), custom_call_target="tpu_custom_call" | custom-call | flops 2147483648 | bytes 10485760 | tf_op jit(solution)/shard_map/rotate/pallas_call | solution.py:331
Async XLA Ops:
  1.9 0.7 %copy-start = (s32[8]{0:T(128)S(1)}, s32[8]{0:T(128)}, u32[]{:S(2)}) copy-start(s32[8]{0:T(128)} %shifts.3) | copy-start | bytes 100

commit v3 on v2

--- a/solution.py
+++ b/solution.py
@@ -26,16 +26,16 @@
 )
 
 
-GROUPS = [(0, 0), (0, 1), (0, 3), (0, 2), (1, None), (3, None), (2, None)]
+GROUPS = [(0, 0)] + list(reversed(OFFSETS))
+SENT = list(range(len(OFFSETS) - SIDE, len(OFFSETS))) + list(range(len(OFFSETS) - SIDE))
 
 
 def product_kernel(
     shifts, widths, steps, state_hbm, left_hbm, right_hbm,
     upd, w_out,
     state, ext0, ext1, left, right, half, total, sibout, sibin, sums, arrived,
-    load_sem, z1_send, z1_recv, f1_send, f1_recv, sib_send, sib_recv,
-    rs_send, rs_recv, ag_send, ag_recv, agf_send, agf_recv,
-    z2_send, z2_recv, z2f_send, z2f_recv,
+    load_sem, z1_recv, f1_recv, sib_recv, rs_recv, ag_recv, agf_recv, z2_recv, z2f_recv,
+    early_send, sib_send, rs_send, ag_send, agf_send, z2_send, z2f_send,
 ):
     ext = (ext0, ext1)
     sectors = lax.axis_size("sec")
@@ -82,28 +82,34 @@
         ext[j][1] = jnp.where(kept, values, 0.0).astype(BF16)
 
     slots = (0, 2)
-    can_send = (z < sectors - 1, z > 0)
-    can_take = (z > 0, z < sectors - 1)
     targets = (up, down)
+    sent_slot = (jnp.where(z == sectors - 1, 3, 1), jnp.where(z == 0, 3, 1))
+
+    @pl.when((z == 0) | (z == sectors - 1))
+    def _():
+        ext0[3] = jnp.zeros((pad, wide), BF16)
+        ext1[3] = jnp.zeros((pad, wide), BF16)
+        upd[3] = jnp.zeros(upd.shape[1:], BF16)
+
     part = pl.ds(pl.multiple_of(core * wide, wide), wide)
     other = pl.ds(pl.multiple_of((1 - core) * wide, wide), wide)
 
     def halo(j, d):
         return remote(
-            ext[j].at[1, part], ext[j].at[slots[d], part],
-            z1_send.at[j, d], z1_recv.at[j, d], targets[d], chan,
+            ext[j].at[sent_slot[d], part], ext[j].at[slots[d], part],
+            early_send, z1_recv.at[j, d], targets[d], chan,
         )
 
     def handed(j, d, rows):
         return remote(
             ext[j].at[slots[d], rows], ext[j].at[slots[d], rows],
-            f1_send.at[j, d], f1_recv.at[j, d], z, sib,
+            early_send, f1_recv.at[j, d], z, sib,
         )
 
     pl.semaphore_wait(barrier, 3 + len(OFFSETS))
     for j in range(2):
         for d in range(2):
-            pl.when(can_send[d])(halo(j, d).start)
+            halo(j, d).start()
     loads = [pltpu.make_async_copy(left_hbm.at[:, 0], left, load_sem.at[1])]
     for j in range(2):
         loads.append(
@@ -114,36 +120,22 @@
     for copy in loads:
         copy.start()
 
-    @pl.when(z == 0)
-    def _():
-        ext0[0] = jnp.zeros((pad, wide), BF16)
-        ext1[0] = jnp.zeros((pad, wide), BF16)
-        upd[0] = jnp.zeros(upd.shape[1:], BF16)
-
-    @pl.when(z == sectors - 1)
-    def _():
-        ext0[2] = jnp.zeros((pad, wide), BF16)
-        ext1[2] = jnp.zeros((pad, wide), BF16)
-        upd[2] = jnp.zeros(upd.shape[1:], BF16)
-
     for copy in loads:
         copy.wait()
 
     def hand_over(j):
         for d in range(2):
-            @pl.when(can_take[d])
-            def _():
-                halo(j, d).wait_recv()
-                handed(j, d, part).start()
+            halo(j, d).wait_recv()
+            handed(j, d, part).start()
 
     def pair_sent(r):
         here = pl.ds(r * CHIPS // 2, CHIPS // 2)
-        return remote(sibout.at[here], sibin.at[here], sib_send.at[r], sib_recv.at[r], z, sib)
+        return remote(sibout.at[here], sibin.at[here], sib_send, sib_recv.at[r], z, sib)
 
     hand_over(0)
     for j in range(2):
         for d in range(2):
-            pl.when(can_take[d])(handed(j, d, other).wait_recv)
+            handed(j, d, other).wait_recv()
         for c in range(channels):
             source = ext[j][1 - shifts[c]]
             half[:, pl.ds(c * wide, wide)] = jnp.dot(
@@ -174,12 +166,6 @@
         there = peer(dy, dx)
         remote(sums.at[there], arrived.at[i], rs_send, rs_recv, z, there * 2 + core).start()
 
-    for j in range(2):
-        for d in range(2):
-            pl.when(can_send[d])(halo(j, d).wait_send)
-            pl.when(can_take[d])(handed(j, d, part).wait_send)
-        pair_sent(j).wait_send()
-
     first = pl.multiple_of(chan * ROWS, ROWS)
     mine = pl.ds(first, ROWS)
     row_ids = first + lax.broadcasted_iota(jnp.int32, (ROWS, pad), 0)
@@ -193,11 +179,7 @@
     upd[1, chip, core] = corrected.astype(BF16)
 
     def group(slot, g, parity):
-        gy, gx = GROUPS[g]
-        if gx is None:
-            rows = pl.ds(pl.multiple_of(lax.rem(y + gy, SIDE) * SIDE, SIDE), SIDE)
-            return upd.at[slot, rows, parity]
-        return upd.at[slot, peer(gy, gx), parity]
+        return upd.at[slot, peer(*GROUPS[g]), parity]
 
     def gathered(i, where):
         dy, dx = OFFSETS[i]
@@ -210,46 +192,37 @@
 
     def to_sibling(g, parity):
         block = group(1, g, parity)
-        return remote(block, block, agf_send.at[g], agf_recv.at[g], z, sib)
+        return remote(block, block, agf_send, agf_recv, z, sib)
 
     def over_z(g, d):
         return remote(
-            group(1, g, core), group(slots[d], g, core),
-            z2_send.at[d, g], z2_recv.at[d, g], targets[d], chan,
+            group(sent_slot[d], g, core), group(slots[d], g, core),
+            z2_send, z2_recv.at[d, GROUPS[g][0]], targets[d], chan,
         )
 
     def z_on(g):
         for d in range(2):
-            pl.when(can_send[d])(over_z(g, d).start)
+            over_z(g, d).start()
 
     z_on(0)
-    for i in range(len(OFFSETS)):
+    for i in SENT:
         gathered(i, chip).start()
     to_sibling(0, core).start()
     for g in range(1, len(GROUPS)):
-        gy, gx = GROUPS[g]
-        for taken in range(SIDE) if gx is None else (gx,):
-            take(gy, taken)
+        take(*GROUPS[g])
         z_on(g)
         to_sibling(g, core).start()
-    wait_bytes(arrived, rs_send)
-    wait_bytes(arrived, ag_send)
-    for g in range(len(GROUPS)):
-        to_sibling(g, 1 - core).wait_recv()
-
-    def halo_handed(gy, d, parity):
+    wait_bytes(upd.at[1, :, 1 - core], agf_recv)
+
+    def chip_row(gy, d, parity):
         rows = pl.ds(pl.multiple_of(lax.rem(y + gy, SIDE) * SIDE, SIDE), SIDE)
-        block = upd.at[slots[d], rows, parity]
-        return remote(block, block, z2f_send.at[d, gy], z2f_recv.at[d, gy], z, sib)
+        return upd.at[slots[d], rows, parity]
 
     def hand_row(gy):
         for d in range(2):
-            @pl.when(can_take[d])
-            def _():
-                for g in range(len(GROUPS)):
-                    if GROUPS[g][0] == gy:
-                        over_z(g, d).wait_recv()
-                halo_handed(gy, d, core).start()
+            block = chip_row(gy, d, core)
+            wait_bytes(block, z2_recv.at[d, gy])
+            remote(block, block, z2f_send, z2f_recv, z, sib).start()
 
     hand_row(0)
     turned = upd[1].reshape(pad, pad).T
@@ -259,16 +232,17 @@
             hand_row(3)
         w_out[c] = jnp.dot(turned, left[c], preferred_element_type=F32).astype(BF16)
     hand_row(2)
-    for g in range(len(GROUPS)):
-        to_sibling(g, core).wait_send()
-        for d in range(2):
-            pl.when(can_send[d])(over_z(g, d).wait_send)
-    for gy in range(SIDE):
-        for d in range(2):
-            @pl.when(can_take[d])
-            def _():
-                halo_handed(gy, d, core).wait_send()
-                halo_handed(gy, d, 1 - core).wait_recv()
+    for sem, ref in (
+        (early_send, left.at[pl.ds(0, 2)]),
+        (sib_send, sibout),
+        (rs_send, arrived),
+        (ag_send, arrived),
+        (agf_send, sums),
+        (z2_send, upd.at[0]),
+        (z2f_send, upd.at[0]),
+    ):
+        wait_bytes(ref, sem)
+    wait_bytes(upd.at[0], z2f_recv)
 
 
 def rotate_kernel(scale, shifts, w, upd, rows_out, out, done, sem):
@@ -291,7 +265,7 @@
 def shards(state_blocks, left_blocks, right_blocks, widths, step_sizes, shifts):
     channels, _, pad, _ = left_blocks.shape
     wide = pad // 2
-    n, m = len(OFFSETS), len(GROUPS)
+    n = len(OFFSETS)
     smem = pl.BlockSpec(memory_space=pltpu.SMEM)
     hbm = pl.BlockSpec(memory_space=pltpu.HBM)
     vmem = pl.BlockSpec(memory_space=pltpu.VMEM)
@@ -301,15 +275,15 @@
         product_kernel,
         name="product",
         out_shape=(
-            jax.ShapeDtypeStruct((3, CHIPS, 2, ROWS, pad), BF16),
+            jax.ShapeDtypeStruct((4, CHIPS, 2, ROWS, pad), BF16),
             jax.ShapeDtypeStruct((channels, pad, pad), BF16),
         ),
         in_specs=[smem] * 3 + [hbm] * 3,
         out_specs=(vmem, vmem),
         scratch_shapes=[
             pltpu.VMEM((pad, pad), BF16),
-            pltpu.VMEM((3, pad, wide), BF16),
-            pltpu.VMEM((3, pad, wide), BF16),
+            pltpu.VMEM((4, pad, wide), BF16),
+            pltpu.VMEM((4, pad, wide), BF16),
             pltpu.VMEM((channels, pad, pad), BF16),
             pltpu.VMEM((2, channels, pad, wide), BF16),
             pltpu.VMEM((pad, channels * wide), BF16),
@@ -318,9 +292,8 @@
             pltpu.VMEM((CHIPS, ROWS, pad), BF16),
             pltpu.VMEM((CHIPS, ROWS, pad), BF16),
             pltpu.VMEM((n, ROWS, pad), BF16),
-            dma((4,)), dma((2, 2)), dma((2, 2)), dma((2, 2)), dma((2, 2)), dma((2,)), dma((2,)),
-            dma(()), dma(()), dma(()), dma((n,)), dma((m,)), dma((m,)),
-            dma((2, m)), dma((2, m)), dma((2, SIDE)), dma((2, SIDE)),
+            dma((4,)), dma((2, 2)), dma((2, 2)), dma((2,)), dma(()), dma((n,)), dma(()), dma((2, SIDE)), dma(()),
+            *[dma(())] * 7,
         ],
         compiler_params=pltpu.CompilerParams(
             collective_id=0, has_side_effects=True, vmem_limit_bytes=32 << 20

time: 49.9 us -> 52.6 us (1.054)
  Pallas kernels: 47.2 us -> 49.8 us
    pallas_call x1, Pallas kernels: 43.4 us -> 46 us  [shards(): pl.pallas_call(product_kernel, name='product', out_shape=(jax.ShapeDtypeS...]
where the time goes in v3:
time: 52.6 us; the launch traced here: 52.4 us
  Pallas kernels  49.8 us (95%)
  between operations  1.94 us (4%)
  local copies, waits for them, and re-layouts  0.65 us (1%)
    pallas_call x1, Pallas kernels, shards(): pl.pallas_call(product_kernel, name='product', out_shape=(jax.ShapeDtypeS...  46 us
    pallas_call x1, Pallas kernels, shards(): pl.pallas_call(functools.partial(rotate_kernel, pad ** (-0.5)), name='rot...  3.77 us

profile of v3, /device:TPU:1, one launch (start us, length us, event | category | flops | bytes accessed | tf_op | source)
XLA Modules:
  0.0 52.4 jit_solution(1657972666171893317)
XLA Ops:
  1.9 0.0 copy-start
  1.9 0.6 %copy-done = s32[8]{0:T(128)S(1)} copy-done((s32[8]{0:T(128)S(1)}, s32[8]{0:T(128)}, u32[]{:S(2)}) %copy-start) | copy-done | bytes 56
  2.6 46.0 %product.1 = (bf16[4,16,2,16,512]{4,3,2,1,0:T(8,128)(2,1)S(1)}, bf16[8,512,512]{2,1,0:T(8,128)(2,1)S(1)}) custom-call(s32[8]{0:T(128)S(1)} %copy-done, s32[1]{0:T(128)S(6)} %copy.8.widths, f32[1]{0:T(128)S(6)} %copy.9.steps, bf16[1,512,512]{2,1,0:T(8,128)(2,1)} %state_hbm.1, bf16[8,1,512,512]{3,2,1,0:T(8,128)(2,1)} %left_hbm.1, ...), custom_call_target="tpu_custom_call" | custom-call | flops 6442450944 | bytes 16777216 | tf_op jit(solution)/shard_map/product/pallas_call | solution.py:274
  48.6 3.8 %rotate.1 = (bf16[1,16,512]{2,1,0:T(8,128)(2,1)}, bf16[8,1,512,512]{3,2,1,0:T(8,128)(2,1)}) custom-call(s32[8]{0:T(128)S(1)} %copy-done, bf16[8,512,512]{2,1,0:T(8,128)(2,1)S(1)} %get-tuple-element.4.w, bf16[4,16,2,16,512]{4,3,2,1,0:T(8,128)(2,1)S(1)} %get-tuple-element.5.upd), custom_call_target="tpu_custom_call" | custom-call | flops 2147483648 | bytes 10485760 | tf_op jit(solution)/shard_map/rotate/pallas_call | solution.py:304
Async XLA Ops:
  1.9 0.7 %copy-start = (s32[8]{0:T(128)S(1)}, s32[8]{0:T(128)}, u32[]{:S(2)}) copy-start(s32[8]{0:T(128)} %shifts.3) | copy-start | bytes 100

commit v4 on v3

--- a/solution.py
+++ b/solution.py
@@ -27,15 +27,15 @@
 
 
 GROUPS = [(0, 0)] + list(reversed(OFFSETS))
-SENT = list(range(len(OFFSETS) - SIDE, len(OFFSETS))) + list(range(len(OFFSETS) - SIDE))
+SENT = list(reversed(range(len(OFFSETS))))
 
 
 def product_kernel(
     shifts, widths, steps, state_hbm, left_hbm, right_hbm,
     upd, w_out,
     state, ext0, ext1, left, right, half, total, sibout, sibin, sums, arrived,
-    load_sem, z1_recv, f1_recv, sib_recv, rs_recv, ag_recv, agf_recv, z2_recv, z2f_recv,
-    early_send, sib_send, rs_send, ag_send, agf_send, z2_send, z2f_send,
+    plane_sem, load_sem, z1_recv, f1_recv, sib_recv, rs_recv, ag_recv, agf_recv, z2_recv, z2f_recv,
+    z1_send, early_send, sib_send, rs_send, ag_send, agf_send, z2_send, z2f_send,
 ):
     ext = (ext0, ext1)
     sectors = lax.axis_size("sec")
@@ -48,7 +48,10 @@
     channels = left_hbm.shape[0]
     pad = state_hbm.shape[1]
     wide = pad // 2
-    up, down = lax.rem(z + 1, sectors), lax.rem(z + sectors - 1, sectors)
+    slots = (0, 2)
+    targets = (lax.rem(z + 1, sectors), lax.rem(z + sectors - 1, sectors))
+    inner = (z < sectors - 1, z > 0)
+    end = (z == 0) | (z == sectors - 1)
 
     def peer(dy, dx):
         return lax.rem(y + dy, SIDE) * SIDE + lax.rem(x + dx, SIDE)
@@ -64,13 +67,14 @@
     load = pltpu.make_async_copy(state_hbm.at[0], state, load_sem.at[0])
     load.start()
     barrier = pltpu.get_barrier_semaphore()
-    for target in (up, down):
-        pl.semaphore_signal(barrier, 1, device_id=(target, chan), device_id_type=MESH)
-    for dy, dx in OFFSETS:
-        pl.semaphore_signal(
-            barrier, 1, device_id=(z, peer(dy, dx) * 2 + core), device_id_type=MESH
-        )
+    for d in range(2):
+        @pl.when(inner[d])
+        def _():
+            pl.semaphore_signal(barrier, 1, device_id=(targets[d], chan), device_id_type=MESH)
     pl.semaphore_signal(barrier, 1, device_id=(z, sib), device_id_type=MESH)
+    for step in range(1, SIDE):
+        for there in (peer(0, step), peer(step, 0)):
+            pl.semaphore_signal(barrier, 1, device_id=(z, there * 2 + core), device_id_type=MESH)
 
     load.wait()
     width = widths[0]
@@ -81,23 +85,20 @@
         values = state[:, pl.ds(j * wide, wide)].astype(F32)
         ext[j][1] = jnp.where(kept, values, 0.0).astype(BF16)
 
-    slots = (0, 2)
-    targets = (up, down)
-    sent_slot = (jnp.where(z == sectors - 1, 3, 1), jnp.where(z == 0, 3, 1))
-
-    @pl.when((z == 0) | (z == sectors - 1))
-    def _():
-        ext0[3] = jnp.zeros((pad, wide), BF16)
-        ext1[3] = jnp.zeros((pad, wide), BF16)
-        upd[3] = jnp.zeros(upd.shape[1:], BF16)
+    for slot, at_end in ((0, z == 0), (2, z == sectors - 1)):
+        @pl.when(at_end)
+        def _():
+            ext0[slot] = jnp.zeros((pad, wide), BF16)
+            ext1[slot] = jnp.zeros((pad, wide), BF16)
+            upd[slot] = jnp.zeros(upd.shape[1:], BF16)
 
     part = pl.ds(pl.multiple_of(core * wide, wide), wide)
     other = pl.ds(pl.multiple_of((1 - core) * wide, wide), wide)
 
     def halo(j, d):
         return remote(
-            ext[j].at[sent_slot[d], part], ext[j].at[slots[d], part],
-            early_send, z1_recv.at[j, d], targets[d], chan,
+            ext[j].at[1, part], ext[j].at[slots[d], part],
+            z1_send.at[j, d], z1_recv.at[j, d], targets[d], chan,
         )
 
     def handed(j, d, rows):
@@ -106,10 +107,18 @@
             early_send, f1_recv.at[j, d], z, sib,
         )
 
-    pl.semaphore_wait(barrier, 3 + len(OFFSETS))
-    for j in range(2):
-        for d in range(2):
-            halo(j, d).start()
+    @pl.when(end)
+    def _():
+        pl.semaphore_wait(barrier, 2 * SIDE)
+
+    @pl.when(jnp.logical_not(end))
+    def _():
+        pl.semaphore_wait(barrier, 2 * SIDE + 1)
+
+    for d in range(2):
+        pl.when(inner[d])(halo(0, d).start)
+    for step in range(1, SIDE):
+        pl.semaphore_signal(plane_sem, 1, device_id=(z, peer(0, step) * 2 + core), device_id_type=MESH)
     loads = [pltpu.make_async_copy(left_hbm.at[:, 0], left, load_sem.at[1])]
     for j in range(2):
         loads.append(
@@ -119,14 +128,20 @@
         )
     for copy in loads:
         copy.start()
+    for d in range(2):
+        pl.when(inner[d])(halo(0, d).wait_send)
+    for d in range(2):
+        pl.when(inner[d])(halo(1, d).start)
 
     for copy in loads:
         copy.wait()
 
     def hand_over(j):
         for d in range(2):
-            halo(j, d).wait_recv()
-            handed(j, d, part).start()
+            @pl.when(inner[1 - d])
+            def _():
+                halo(j, d).wait_recv()
+                handed(j, d, part).start()
 
     def pair_sent(r):
         here = pl.ds(r * CHIPS // 2, CHIPS // 2)
@@ -135,7 +150,7 @@
     hand_over(0)
     for j in range(2):
         for d in range(2):
-            handed(j, d, other).wait_recv()
+            pl.when(inner[1 - d])(handed(j, d, other).wait_recv)
         for c in range(channels):
             source = ext[j][1 - shifts[c]]
             half[:, pl.ds(c * wide, wide)] = jnp.dot(
@@ -162,6 +177,7 @@
         pair = total[here, core] + sibin[here].astype(F32)
         sums[here] = pair.astype(BF16)
         total[here, core] = pair
+    pl.semaphore_wait(plane_sem, SIDE - 1)
     for i, (dy, dx) in enumerate(OFFSETS):
         there = peer(dy, dx)
         remote(sums.at[there], arrived.at[i], rs_send, rs_recv, z, there * 2 + core).start()
@@ -190,28 +206,24 @@
         i = OFFSETS.index(((SIDE - gy) % SIDE, (SIDE - gx) % SIDE))
         gathered(i, peer(gy, gx)).wait_recv()
 
-    def to_sibling(g, parity):
-        block = group(1, g, parity)
-        return remote(block, block, agf_send, agf_recv, z, sib)
-
     def over_z(g, d):
         return remote(
-            group(sent_slot[d], g, core), group(slots[d], g, core),
+            group(1, g, core), group(slots[d], g, core),
             z2_send, z2_recv.at[d, GROUPS[g][0]], targets[d], chan,
         )
 
     def z_on(g):
         for d in range(2):
-            over_z(g, d).start()
+            pl.when(inner[d])(over_z(g, d).start)
 
     z_on(0)
     for i in SENT:
         gathered(i, chip).start()
-    to_sibling(0, core).start()
     for g in range(1, len(GROUPS)):
         take(*GROUPS[g])
         z_on(g)
-        to_sibling(g, core).start()
+    own_rows = upd.at[1, :, core]
+    remote(own_rows, own_rows, agf_send, agf_recv, z, sib).start()
     wait_bytes(upd.at[1, :, 1 - core], agf_recv)
 
     def chip_row(gy, d, parity):
@@ -220,9 +232,11 @@
 
     def hand_row(gy):
         for d in range(2):
-            block = chip_row(gy, d, core)
-            wait_bytes(block, z2_recv.at[d, gy])
-            remote(block, block, z2f_send, z2f_recv, z, sib).start()
+            @pl.when(inner[1 - d])
+            def _():
+                block = chip_row(gy, d, core)
+                wait_bytes(block, z2_recv.at[d, gy])
+                remote(block, block, z2f_send, z2f_recv, z, sib).start()
 
     hand_row(0)
     turned = upd[1].reshape(pad, pad).T
@@ -232,17 +246,23 @@
             hand_row(3)
         w_out[c] = jnp.dot(turned, left[c], preferred_element_type=F32).astype(BF16)
     hand_row(2)
-    for sem, ref in (
-        (early_send, left.at[pl.ds(0, 2)]),
-        (sib_send, sibout),
-        (rs_send, arrived),
-        (ag_send, arrived),
-        (agf_send, sums),
-        (z2_send, upd.at[0]),
-        (z2f_send, upd.at[0]),
-    ):
+    for sem, ref in ((sib_send, sibout), (rs_send, arrived), (ag_send, arrived), (agf_send, sums)):
         wait_bytes(ref, sem)
-    wait_bytes(upd.at[0], z2f_recv)
+
+    for d in range(2):
+        pl.when(inner[d])(halo(1, d).wait_send)
+
+    @pl.when(end)
+    def _():
+        wait_bytes(sums, early_send)
+        for sem in (z2_send, z2f_send, z2f_recv):
+            wait_bytes(sums, sem)
+
+    @pl.when(jnp.logical_not(end))
+    def _():
+        wait_bytes(left.at[0], early_send)
+        for sem in (z2_send, z2f_send, z2f_recv):
+            wait_bytes(left.at[0], sem)
 
 
 def rotate_kernel(scale, shifts, w, upd, rows_out, out, done, sem):
@@ -270,20 +290,21 @@
     hbm = pl.BlockSpec(memory_space=pltpu.HBM)
     vmem = pl.BlockSpec(memory_space=pltpu.VMEM)
     dma = pltpu.SemaphoreType.DMA
+    scalars = pltpu.with_memory_space_constraint(shifts, pltpu.HBM)
     blocks = (pltpu.with_memory_space_constraint(a, pltpu.HBM) for a in (state_blocks, left_blocks, right_blocks))
     upd, turned = pl.pallas_call(
         product_kernel,
         name="product",
         out_shape=(
-            jax.ShapeDtypeStruct((4, CHIPS, 2, ROWS, pad), BF16),
+            jax.ShapeDtypeStruct((3, CHIPS, 2, ROWS, pad), BF16),
             jax.ShapeDtypeStruct((channels, pad, pad), BF16),
         ),
         in_specs=[smem] * 3 + [hbm] * 3,
         out_specs=(vmem, vmem),
         scratch_shapes=[
             pltpu.VMEM((pad, pad), BF16),
-            pltpu.VMEM((4, pad, wide), BF16),
-            pltpu.VMEM((4, pad, wide), BF16),
+            pltpu.VMEM((3, pad, wide), BF16),
+            pltpu.VMEM((3, pad, wide), BF16),
             pltpu.VMEM((channels, pad, pad), BF16),
             pltpu.VMEM((2, channels, pad, wide), BF16),
             pltpu.VMEM((pad, channels * wide), BF16),
@@ -292,14 +313,14 @@
             pltpu.VMEM((CHIPS, ROWS, pad), BF16),
             pltpu.VMEM((CHIPS, ROWS, pad), BF16),
             pltpu.VMEM((n, ROWS, pad), BF16),
-            dma((4,)), dma((2, 2)), dma((2, 2)), dma((2,)), dma(()), dma((n,)), dma(()), dma((2, SIDE)), dma(()),
-            *[dma(())] * 7,
+            pltpu.SemaphoreType.REGULAR, dma((4,)), dma((2, 2)), dma((2, 2)), dma((2,)), dma(()), dma((n,)), dma(()), dma((2, SIDE)), dma(()),
+            dma((2, 2)), *[dma(())] * 7,
         ],
         compiler_params=pltpu.CompilerParams(
             collective_id=0, has_side_effects=True, vmem_limit_bytes=32 << 20
         ),
         cost_estimate=pl.CostEstimate(flops=6 << 30, bytes_accessed=16 << 20, transcendentals=0),
-    )(shifts, widths, step_sizes, *blocks)
+    )(scalars, widths, step_sizes, *blocks)
 
     rows, new_left = pl.pallas_call(
         functools.partial(rotate_kernel, pad ** (-0.5)),
@@ -316,7 +337,7 @@
         ],
         compiler_params=pltpu.CompilerParams(vmem_limit_bytes=16 << 20),
         cost_estimate=pl.CostEstimate(flops=2 << 30, bytes_accessed=10 << 20, transcendentals=0),
-    )(shifts, turned, upd)
+    )(scalars, turned, upd)
     return rows, new_left
 
 

time: 52.6 us -> 46.8 us (0.89)
  Pallas kernels: 49.8 us -> 44.4 us
  local copies, waits for them, and re-layouts: 0.65 us -> 0 us
    pallas_call x1, Pallas kernels: 46 us -> 40.5 us  [shards(): pl.pallas_call(product_kernel, name='product', out_shape=(jax.ShapeDtypeS...]
    unnamed x2 -> x0, local copies, waits for them, and re-layouts: 0.65 us -> none
where the time goes in v4:
time: 46.8 us; the launch traced here: 46.3 us
  Pallas kernels  44.4 us (95%)
  between operations  1.93 us (4%)
    pallas_call x1, Pallas kernels, shards(): pl.pallas_call(product_kernel, name='product', out_shape=(jax.ShapeDtypeS...  40.5 us
    pallas_call x1, Pallas kernels, shards(): pl.pallas_call(functools.partial(rotate_kernel, pad ** (-0.5)), name='rot...  3.89 us

profile of v4, /device:TPU:1, one launch (start us, length us, event | category | flops | bytes accessed | tf_op | source)
XLA Modules:
  0.0 46.3 jit_solution(4768744530470918197)
XLA Ops:
  1.9 40.5 %product.1 = (bf16[3,16,2,16,512]{4,3,2,1,0:T(8,128)(2,1)S(1)}, bf16[8,512,512]{2,1,0:T(8,128)(2,1)S(1)}) custom-call(s32[8]{0:T(128)} %shifts.3, s32[1]{0:T(128)S(6)} %copy.8.widths, f32[1]{0:T(128)S(6)} %copy.9.steps, bf16[1,512,512]{2,1,0:T(8,128)(2,1)} %state_hbm.1, bf16[8,1,512,512]{3,2,1,0:T(8,128)(2,1)} %left_hbm.1, bf16[8,1,512,512]{3,2,1,0:T(8,128)(2,1)} %right_hbm.1), custom_call_target="tpu_custom_call" | custom-call | flops 6442450944 | bytes 16777216 | tf_op jit(solution)/shard_map/product/pallas_call | solution.py:295
  42.4 3.9 %rotate.1 = (bf16[1,16,512]{2,1,0:T(8,128)(2,1)}, bf16[8,1,512,512]{3,2,1,0:T(8,128)(2,1)}) custom-call(s32[8]{0:T(128)} %shifts.3, bf16[8,512,512]{2,1,0:T(8,128)(2,1)S(1)} %get-tuple-element.4.w, bf16[3,16,2,16,512]{4,3,2,1,0:T(8,128)(2,1)S(1)} %get-tuple-element.5.upd), custom_call_target="tpu_custom_call" | custom-call | flops 2147483648 | bytes 10485760 | tf_op jit(solution)/shard_map/rotate/pallas_call | solution.py:325

commit v5 on v4

--- a/solution.py
+++ b/solution.py
@@ -171,16 +171,21 @@
                 sibout[here] = total[here, 1 - core].astype(BF16)
                 pair_sent(r).start()
 
+    pl.semaphore_wait(plane_sem, SIDE - 1)
     for r in range(2):
         here = pl.ds(r * CHIPS // 2, CHIPS // 2)
         pair_sent(r).wait_recv()
         pair = total[here, core] + sibin[here].astype(F32)
         sums[here] = pair.astype(BF16)
         total[here, core] = pair
-    pl.semaphore_wait(plane_sem, SIDE - 1)
-    for i, (dy, dx) in enumerate(OFFSETS):
-        there = peer(dy, dx)
-        remote(sums.at[there], arrived.at[i], rs_send, rs_recv, z, there * 2 + core).start()
+        for i, (dy, dx) in enumerate(OFFSETS):
+            there = peer(dy, dx)
+
+            @pl.when(there // (CHIPS // 2) == r)
+            def _():
+                remote(
+                    sums.at[there], arrived.at[i], rs_send, rs_recv, z, there * 2 + core
+                ).start()
 
     first = pl.multiple_of(chan * ROWS, ROWS)
     mine = pl.ds(first, ROWS)
@@ -238,14 +243,11 @@
                 wait_bytes(block, z2_recv.at[d, gy])
                 remote(block, block, z2f_send, z2f_recv, z, sib).start()
 
-    hand_row(0)
+    for gy in (0, 1, 3, 2):
+        hand_row(gy)
     turned = upd[1].reshape(pad, pad).T
     for c in range(channels):
-        if c == channels // 2:
-            hand_row(1)
-            hand_row(3)
         w_out[c] = jnp.dot(turned, left[c], preferred_element_type=F32).astype(BF16)
-    hand_row(2)
     for sem, ref in ((sib_send, sibout), (rs_send, arrived), (ag_send, arrived), (agf_send, sums)):
         wait_bytes(ref, sem)
 

time: 46.8 us -> 45.7 us (0.976)
  the two profiles are of different devices: /device:TPU:1 before, /device:TPU:64 now
where the time goes in v5:
time: 45.7 us; the launch traced here: 45.5 us
  Pallas kernels  43.6 us (95%)
  between operations  1.93 us (4%)
    pallas_call x1, Pallas kernels, shards(): pl.pallas_call(product_kernel, name='product', out_shape=(jax.ShapeDtypeS...  39.7 us
    pallas_call x1, Pallas kernels, shards(): pl.pallas_call(functools.partial(rotate_kernel, pad ** (-0.5)), name='rot...  3.89 us

profile of v5, /device:TPU:64, one launch (start us, length us, event | category | flops | bytes accessed | tf_op | source)
XLA Modules:
  0.0 45.5 jit_solution(2165269502481984514)
XLA Ops:
  1.9 39.7 %product.1 = (bf16[3,16,2,16,512]{4,3,2,1,0:T(8,128)(2,1)S(1)}, bf16[8,512,512]{2,1,0:T(8,128)(2,1)S(1)}) custom-call(s32[8]{0:T(128)} %shifts.3, s32[1]{0:T(128)S(6)} %copy.8.widths, f32[1]{0:T(128)S(6)} %copy.9.steps, bf16[1,512,512]{2,1,0:T(8,128)(2,1)} %state_hbm.1, bf16[8,1,512,512]{3,2,1,0:T(8,128)(2,1)} %left_hbm.1, bf16[8,1,512,512]{3,2,1,0:T(8,128)(2,1)} %right_hbm.1), custom_call_target="tpu_custom_call" | custom-call | flops 6442450944 | bytes 16777216 | tf_op jit(solution)/shard_map/product/pallas_call | solution.py:297
  41.7 3.9 %rotate.1 = (bf16[1,16,512]{2,1,0:T(8,128)(2,1)}, bf16[8,1,512,512]{3,2,1,0:T(8,128)(2,1)}) custom-call(s32[8]{0:T(128)} %shifts.3, bf16[8,512,512]{2,1,0:T(8,128)(2,1)S(1)} %get-tuple-element.4.w, bf16[3,16,2,16,512]{4,3,2,1,0:T(8,128)(2,1)S(1)} %get-tuple-element.5.upd), custom_call_target="tpu_custom_call" | custom-call | flops 2147483648 | bytes 10485760 | tf_op jit(solution)/shard_map/rotate/pallas_call | solution.py:327

commit v6 on v5

--- a/solution.py
+++ b/solution.py
@@ -76,6 +76,15 @@
         for there in (peer(0, step), peer(step, 0)):
             pl.semaphore_signal(barrier, 1, device_id=(z, there * 2 + core), device_id_type=MESH)
 
+    loads = [pltpu.make_async_copy(left_hbm.at[:, 0], left, load_sem.at[1])]
+    for j in range(2):
+        loads.append(
+            pltpu.make_async_copy(
+                right_hbm.at[:, 0, :, pl.ds(j * wide, wide)], right.at[j], load_sem.at[2 + j]
+            )
+        )
+    for copy in loads:
+        copy.start()
     load.wait()
     width = widths[0]
     rows_at = lax.broadcasted_iota(jnp.int32, (pad, wide), 0)
@@ -119,15 +128,6 @@
         pl.when(inner[d])(halo(0, d).start)
     for step in range(1, SIDE):
         pl.semaphore_signal(plane_sem, 1, device_id=(z, peer(0, step) * 2 + core), device_id_type=MESH)
-    loads = [pltpu.make_async_copy(left_hbm.at[:, 0], left, load_sem.at[1])]
-    for j in range(2):
-        loads.append(
-            pltpu.make_async_copy(
-                right_hbm.at[:, 0, :, pl.ds(j * wide, wide)], right.at[j], load_sem.at[2 + j]
-            )
-        )
-    for copy in loads:
-        copy.start()
     for d in range(2):
         pl.when(inner[d])(halo(0, d).wait_send)
     for d in range(2):
@@ -156,6 +156,8 @@
             half[:, pl.ds(c * wide, wide)] = jnp.dot(
                 left[c], source, preferred_element_type=F32
             ).astype(BF16)
+        if j == 0:
+            hand_over(1)
         for r in range(2):
             beside = jnp.concatenate([right[j, c] for c in range(channels)], axis=1)
             value = lax.dot_general(
@@ -164,8 +166,6 @@
             here = pl.ds(r * CHIPS // 2, CHIPS // 2)
             if j == 0:
                 total[here] = value
-                if r == 0:
-                    hand_over(1)
             else:
                 total[here] = total[here] + value
                 sibout[here] = total[here, 1 - core].astype(BF16)

time: 45.7 us -> 45 us (0.985)
  Pallas kernels: 43.6 us -> 43 us
    pallas_call x1, Pallas kernels: 39.7 us -> 39.1 us  [shards(): pl.pallas_call(product_kernel, name='product', out_shape=(jax.ShapeDtypeS...]
where the time goes in v6:
time: 45 us; the launch traced here: 44.9 us
  Pallas kernels  43 us (96%)
  between operations  1.93 us (4%)
    pallas_call x1, Pallas kernels, shards(): pl.pallas_call(product_kernel, name='product', out_shape=(jax.ShapeDtypeS...  39.1 us
    pallas_call x1, Pallas kernels, shards(): pl.pallas_call(functools.partial(rotate_kernel, pad ** (-0.5)), name='rot...  3.89 us

profile of v6, /device:TPU:64, one launch (start us, length us, event | category | flops | bytes accessed | tf_op | source)
XLA Modules:
  0.0 44.9 jit_solution(12120327321470313319)
XLA Ops:
  1.9 39.1 %product.1 = (bf16[3,16,2,16,512]{4,3,2,1,0:T(8,128)(2,1)S(1)}, bf16[8,512,512]{2,1,0:T(8,128)(2,1)S(1)}) custom-call(s32[8]{0:T(128)} %shifts.3, s32[1]{0:T(128)S(6)} %copy.8.widths, f32[1]{0:T(128)S(6)} %copy.9.steps, bf16[1,512,512]{2,1,0:T(8,128)(2,1)} %state_hbm.1, bf16[8,1,512,512]{3,2,1,0:T(8,128)(2,1)} %left_hbm.1, bf16[8,1,512,512]{3,2,1,0:T(8,128)(2,1)} %right_hbm.1), custom_call_target="tpu_custom_call" | custom-call | flops 6442450944 | bytes 16777216 | tf_op jit(solution)/shard_map/product/pallas_call | solution.py:297
  41.0 3.9 %rotate.1 = (bf16[1,16,512]{2,1,0:T(8,128)(2,1)}, bf16[8,1,512,512]{3,2,1,0:T(8,128)(2,1)}) custom-call(s32[8]{0:T(128)} %shifts.3, bf16[8,512,512]{2,1,0:T(8,128)(2,1)S(1)} %get-tuple-element.4.w, bf16[3,16,2,16,512]{4,3,2,1,0:T(8,128)(2,1)S(1)} %get-tuple-element.5.upd), custom_call_target="tpu_custom_call" | custom-call | flops 2147483648 | bytes 10485760 | tf_op jit(solution)/shard_map/rotate/pallas_call | solution.py:327
